TPU v7x, 512 devices: a whole 4x4x16 slice. The times are simulated.
512 devices in a mesh: warp: 32 (over z_hi, x, core), weft: 16 (over y, z_lo).
Axes of the slice: x: 4, y: 4, z: 16 (z_hi: 4, z_lo: 4; z = z_hi * 4 + z_lo), core: 2. Of those that a mesh axis runs over, the one named last changes fastest.
Arguments:
- fabric_state: float32 [1, 8, 256, 2048], P(None, None, 'warp', 'weft'), may hold values from -3 to 3
- final_adjoint: float32 [1, 8, 256, 2048], P(None, None, 'warp', 'weft'), may hold values from -6 to 6
- stiffness: float32 [2, 256, 2048], P(None, 'warp', 'weft'), may hold values from 0.5 to 2
- pinned: int32 [1, 256, 2048], P(None, 'warp', 'weft'), may hold values 0 or 1
- weave_codes: int32 [256, 2048], P('warp', 'weft'), may hold values from 0 to 3
- first_weight: bfloat16 [12, 256], replicated, may hold values from -1.75 to 1.75
- second_weight: bfloat16 [256, 256], replicated, may hold values from -0.375 to 0.375
- third_weight: bfloat16 [256, 2], replicated, may hold values from -0.375 to 0.375
Outputs:
- final_state: float32 [1, 8, 256, 2048], P(None, None, 'warp', 'weft')
- state_adjoint: float32 [1, 8, 256, 2048], P(None, None, 'warp', 'weft')
- first_grad: float32 [12, 256], replicated
- second_grad: float32 [256, 256], replicated
- third_grad: float32 [256, 2], replicated
Inputs may be any that keep to these rules, and one draw needn't show every extreme that they name: `pinned`: 1 marks a crossing held fixed in that drape condition. `weave_codes`: bit 0 tells whether the warp passes over, bit 1 the weave's second pattern bit.
All inputs are finite; a program needn't handle non-finite values. No bound on the sum of `pinned` on one device may be relied on, other than what follows from the above.
Results may differ from a plain program's by a relative error of at most 0.0049.
Values sent between devices are 32-bit elements; how exact they have to be, the bound alone decides.
No kernel may reach another device: no remote copies, remote signals or barrier semaphores. Data moves between devices by JAX's collectives and lax.ppermute only.
A program may use at most 64 MiB of HBM per device.

v0:
```python
import jax
import jax.numpy as jnp
from jax import lax
from jax.sharding import PartitionSpec as P

SUBSTEPS = 3


time_step = 0.25
damping = 0.9
bending = 0.25
coupling = 0.5
sliding = 0.5
gravity = 0.3


def with_halo(block, sides, width):
    for axis, dim in sides:
        count = lax.axis_size(axis)
        forward = [(i, i + 1) for i in range(count - 1)]
        backward = [(target, source) for source, target in forward]
        low = lax.ppermute(
            lax.slice_in_dim(block, block.shape[dim] - width, None, axis=dim), axis, forward
        )
        high = lax.ppermute(lax.slice_in_dim(block, 0, width, axis=dim), axis, backward)
        block = jnp.concatenate([low, block, high], axis=dim)
    return block


def center(padded):
    return padded[..., 2:-2, 2:-2]


def laplace_rows(padded):
    return padded[..., 3:-1, 2:-2] + padded[..., 1:-3, 2:-2] - 2.0 * padded[..., 2:-2, 2:-2]


def laplace_columns(padded):
    return padded[..., 2:-2, 3:-1] + padded[..., 2:-2, 1:-3] - 2.0 * padded[..., 2:-2, 2:-2]


def slope_rows(padded):
    return 0.5 * (padded[..., 3:-1, 2:-2] - padded[..., 1:-3, 2:-2])


def slope_columns(padded):
    return 0.5 * (padded[..., 2:-2, 3:-1] - padded[..., 2:-2, 1:-3])


def bend_rows(padded):
    return (
        padded[..., 4:, 2:-2]
        - 4.0 * padded[..., 3:-1, 2:-2]
        + 6.0 * padded[..., 2:-2, 2:-2]
        - 4.0 * padded[..., 1:-3, 2:-2]
        + padded[..., :-4, 2:-2]
    )


def bend_columns(padded):
    return (
        padded[..., 2:-2, 4:]
        - 4.0 * padded[..., 2:-2, 3:-1]
        + 6.0 * padded[..., 2:-2, 2:-2]
        - 4.0 * padded[..., 2:-2, 1:-3]
        + padded[..., 2:-2, :-4]
    )


def features(padded, weave_codes):
    inner = center(padded)
    conditions = padded.shape[0]
    first_sign = (2 * (weave_codes % 2) - 1).astype(jnp.float32)
    second_sign = (2 * (weave_codes // 2) - 1).astype(jnp.float32)
    shape = (conditions,) + first_sign.shape
    fields = [
        inner[:, 6],
        inner[:, 7],
        inner[:, 3],
        inner[:, 4],
        inner[:, 5],
        laplace_rows(padded[:, 6]),
        laplace_columns(padded[:, 7]),
        slope_rows(padded[:, 0]),
        slope_columns(padded[:, 1]),
        inner[:, 2],
        jnp.broadcast_to(first_sign, shape),
        jnp.broadcast_to(second_sign, shape),
    ]
    return jnp.stack(fields, axis=1)


def advance(padded, stiffness, free, friction):
    inner = center(padded)
    place = padded[:, 0:3]
    force = (
        stiffness[0] * laplace_rows(place)
        + stiffness[1] * laplace_columns(place)
        - bending * (bend_rows(place) + bend_columns(place))
    )
    normal = jnp.zeros_like(inner[:, 0]) - gravity
    extra = jnp.stack(
        [coupling * slope_rows(padded[:, 6]), coupling * slope_columns(padded[:, 7]), normal],
        axis=1,
    )
    force = force + extra
    velocity = free[:, None] * (damping * inner[:, 3:6] + time_step * force)
    place_new = inner[:, 0:3] + time_step * velocity
    slide_rate = (
        sliding * jnp.stack([laplace_rows(padded[:, 6]), laplace_columns(padded[:, 7])], axis=1)
        - friction
    )
    slide_new = inner[:, 6:8] + time_step * slide_rate
    return jnp.concatenate([place_new, velocity, slide_new], axis=1)


def flatten(field):
    return jnp.moveaxis(field, 1, 0).reshape(field.shape[1], -1)


def unflatten(flat, conditions, local_rows, local_columns):
    return jnp.moveaxis(flat.reshape(flat.shape[0], conditions, local_rows, local_columns), 0, 1)


def blocks_of(flat, width):
    return jnp.moveaxis(flat.reshape(flat.shape[0], -1, width), 1, 0)


def joined(blocked):
    return jnp.moveaxis(blocked, 0, 1).reshape(blocked.shape[1], -1)


def contract(left, right):
    return lax.dot_general(
        left, right, (((0,), (0,)), ((), ())), preferred_element_type=jnp.float32
    )


def outer_sum(left, right):
    return lax.dot_general(
        left, right, (((1,), (1,)), ((), ())), preferred_element_type=jnp.float32
    )


def hidden_layers(first_weight, second_weight, inputs):
    pre_first = contract(first_weight, inputs)
    act_first = jax.nn.silu(pre_first).astype(jnp.bfloat16)
    pre_second = contract(second_weight, act_first)
    act_second = jax.nn.silu(pre_second).astype(jnp.bfloat16)
    return (pre_first, act_first, pre_second, act_second)


def silu_slope(pre):
    sigmoid_value = jax.nn.sigmoid(pre)
    return sigmoid_value * (1.0 + pre * (1.0 - sigmoid_value))


def friction_block(weights, inputs):
    first_weight, second_weight, third_weight = weights
    layers = hidden_layers(first_weight, second_weight, inputs)
    return contract(third_weight, layers[3])


def friction_back(weights, inputs, upstream):
    first_weight, second_weight, third_weight = weights
    pre_first, act_first, pre_second, act_second = hidden_layers(
        first_weight, second_weight, inputs
    )
    upstream_low = upstream.astype(jnp.bfloat16)
    grad_third = outer_sum(act_second, upstream_low)
    back_second = (
        jnp.dot(third_weight, upstream_low, preferred_element_type=jnp.float32)
        * silu_slope(pre_second)
    ).astype(jnp.bfloat16)
    grad_second = outer_sum(act_first, back_second)
    back_first = (
        jnp.dot(second_weight, back_second, preferred_element_type=jnp.float32)
        * silu_slope(pre_first)
    ).astype(jnp.bfloat16)
    grad_first = outer_sum(inputs, back_first)
    feature_grad = jnp.dot(first_weight, back_first, preferred_element_type=jnp.float32)
    return (feature_grad, (grad_first, grad_second, grad_third))


def friction_all(weights, inputs, width):

    def one_block(piece):
        return friction_block(weights, piece)

    return joined(lax.map(one_block, blocks_of(inputs, width)))


def friction_grads(weights, inputs, upstream, width):
    start = tuple((jnp.zeros(weight.shape, jnp.float32) for weight in weights))

    def one_block(carry, pair):
        feature_grad, grads = friction_back(weights, pair[0], pair[1])
        return ((carry[0] + grads[0], carry[1] + grads[1], carry[2] + grads[2]), feature_grad)

    totals, feature_blocks = lax.scan(
        one_block, start, (blocks_of(inputs, width), blocks_of(upstream, width))
    )
    return (joined(feature_blocks), totals)


def adjoint_local(adjoint, free, inputs, weights, width):
    conditions, _, local_rows, local_columns = adjoint.shape
    total_velocity = adjoint[:, 3:6] + time_step * adjoint[:, 0:3]
    force_adjoint = (free * time_step)[:, None] * total_velocity
    slide_adjoint = adjoint[:, 6:8]
    upstream = flatten(-time_step * slide_adjoint)
    feature_flat, grads = friction_grads(weights, inputs, upstream, width)
    feature_adjoint = unflatten(feature_flat, conditions, local_rows, local_columns)
    carried = jnp.concatenate(
        [
            force_adjoint,
            time_step * sliding * slide_adjoint + feature_adjoint[:, 5:7],
            feature_adjoint[:, 7:9],
        ],
        axis=1,
    )
    kept = (
        adjoint[:, 0:3],
        (free * damping)[:, None] * total_velocity + feature_adjoint[:, 2:5],
        slide_adjoint + feature_adjoint[:, 0:2],
        feature_adjoint[:, 9],
    )
    return (carried, kept, grads)


def adjoint_finish(padded, stiff_pad, kept):
    place_adjoint, velocity_adjoint, slide_adjoint, normal_adjoint = kept
    force_pad = padded[:, 0:3]
    place = (
        place_adjoint
        + laplace_rows(stiff_pad[0] * force_pad)
        + laplace_columns(stiff_pad[1] * force_pad)
        - bending * (bend_rows(force_pad) + bend_columns(force_pad))
    )
    place = place + jnp.stack(
        [-slope_rows(padded[:, 5]), -slope_columns(padded[:, 6]), normal_adjoint], axis=1
    )
    slide = slide_adjoint + jnp.stack(
        [
            laplace_rows(padded[:, 3]) - coupling * slope_rows(padded[:, 0]),
            laplace_columns(padded[:, 4]) - coupling * slope_columns(padded[:, 1]),
        ],
        axis=1,
    )
    return jnp.concatenate([place, velocity_adjoint, slide], axis=1)


def spread_field(current):
    return with_halo(current, (("warp", 2), ("weft", 3)), 2)


def spread_adjoint(carried):
    return with_halo(carried, (("warp", 2), ("weft", 3)), 2)


def shards(
    fabric_state,
    final_adjoint,
    stiffness,
    pinned,
    weave_codes,
    first_weight,
    second_weight,
    third_weight,
):
    conditions, local_rows, local_columns = pinned.shape
    cells = conditions * local_rows * local_columns
    width = min(512, cells)
    weights = (first_weight, second_weight, third_weight)
    free = 1.0 - pinned.astype(jnp.float32)
    saved = []
    current = fabric_state
    for substep in range(SUBSTEPS):
        padded = spread_field(current)
        inputs = flatten(features(padded, weave_codes)).astype(jnp.bfloat16)
        saved.append(inputs)
        friction = unflatten(
            friction_all(weights, inputs, width), conditions, local_rows, local_columns
        )
        current = advance(padded, stiffness, free, friction)
    stiff_pad = with_halo(stiffness, (("warp", 1), ("weft", 2)), 2)
    adjoint = final_adjoint
    collected = []
    for substep in reversed(range(SUBSTEPS)):
        carried, kept, grads = adjoint_local(adjoint, free, saved[substep], weights, width)
        collected.append(grads)
        adjoint = adjoint_finish(spread_adjoint(carried), stiff_pad, kept)
    local_totals = collected[0]
    for later in collected[1:]:
        local_totals = (
            local_totals[0] + later[0],
            local_totals[1] + later[1],
            local_totals[2] + later[2],
        )
    totals = lax.psum((local_totals[0], local_totals[1], local_totals[2]), ("warp", "weft"))
    scale = float(cells * lax.axis_size("warp") * lax.axis_size("weft")) ** (-0.5)
    return (current, adjoint, totals[0] * scale, totals[1] * scale, totals[2] * scale)


def solution(mesh):
    placed = (
        P(None, None, "warp", "weft"),
        P(None, None, "warp", "weft"),
        P(None, "warp", "weft"),
        P(None, "warp", "weft"),
        P("warp", "weft"),
        P(),
        P(),
        P(),
    )
    return jax.shard_map(
        shards,
        mesh=mesh,
        in_specs=placed,
        out_specs=(P(None, None, "warp", "weft"), P(None, None, "warp", "weft"), P(), P(), P()),
        check_vma=False,
    )
```

profile of v0, /device:TPU:1, one launch (start us, length us, event | category | flops | bytes accessed | tf_op | source)
XLA Modules:
  0.0 748.9 jit_solution(16129546594037095739)
XLA Ops:
  8.0 4.5 collective-permute-start.12
  12.5 5.6 collective-permute-start.13
  18.1 0.8 fusion.279
  18.9 1.9 collective-permute-start.1
  20.9 2.4 collective-permute-start
  25.0 0.8 collective-permute-done
  25.9 1.6 collective-permute-start.3
  27.5 1.3 collective-permute-start.2
  28.9 3.9 collective-permute-done.2
  34.1 1.5 while.81
  35.8 4.6 collective-permute-start.5
  40.4 1.9 collective-permute-start.4
  42.4 3.0 collective-permute-done.4
  45.5 3.1 collective-permute-start.7
  48.6 1.3 collective-permute-start.6
  50.0 4.1 collective-permute-start.14
  54.1 1.3 collective-permute-start.15
  56.2 1.5 while.82
  57.9 2.7 collective-permute-start.9
  60.6 1.9 collective-permute-start.8
  62.6 2.9 collective-permute-done.8
  65.6 5.2 collective-permute-start.11
  70.9 1.3 collective-permute-start.10
  72.3 3.8 collective-permute-done.10
  76.7 4.4 while.84
  81.3 10.8 %collective-permute-start.16 = (f32[1,7,2,128]{3,2,1,0:T(2,128)S(1)}, f32[1,7,2,128]{3,2,1,0:T(2,128)S(1)}, u32[]{:S(2)}, u32[]{:S(2)}) collective-permute-start(f32[1,7,2,128]{3,2,1,0:T(2,128)S(1)} %get-tuple-element.562), channel_id=1, source_target_pairs={{0,16},{16,32},{32,48},{48,64},{64,80},{80,96},{96,112},{112,128},... | collective-permute-start | bytes 21512 | tf_op jit(solution)/shard_map/ppermute | solution.py:22
  92.1 1.9 collective-permute-start.17
  94.1 1.5 while.83
  95.6 6.2 collective-permute-done.17
  101.9 4.6 collective-permute-start.18
  106.5 1.3 collective-permute-start.19
  108.0 6.5 collective-permute-done.19
  114.9 4.4 while.85
  120.5 4.6 collective-permute-start.20
  125.0 1.9 collective-permute-start.21
  127.0 8.2 %collective-permute-done.21 = f32[1,7,2,128]{3,2,1,0:T(2,128)S(1)} collective-permute-done((f32[1,7,2,128]{3,2,1,0:T(2,128)S(1)}, f32[1,7,2,128]{3,2,1,0:T(2,128)S(1)}, u32[]{:S(2)}, u32[]{:S(2)}) %collective-permute-start.21) | collective-permute-done | bytes 7200 | tf_op jit(solution)/shard_map/ppermute | solution.py:25
  135.3 6.0 collective-permute-start.22
  141.3 1.3 collective-permute-start.23
  143.3 3.6 collective-permute-done.23
  147.3 4.4 while.86
  152.9 4.3 collective-permute-start.24
  157.2 1.9 collective-permute-start.25
  159.1 132.6 %all-reduce = (f32[12,256]{1,0:T(8,128)S(1)}, f32[256,2]{0,1:T(2,128)S(1)}) all-reduce(f32[12,256]{1,0:T(8,128)S(1)} %add_add_fusion.1, f32[256,2]{0,1:T(2,128)S(1)} %add_add_fusion.2), channel_id=1, replica_groups=mesh['warp'=32,'weft'=16] {'warp','weft'}, use_global_device_ids=true, to_apply=%region_12.13 | all-reduce | flops 3584 | bytes 28672 | tf_op jit(solution)/shard_map/psum | solution.py:300
  293.2 1.6 collective-permute-start.26
  294.8 1.3 collective-permute-start.27
  296.7 3.6 collective-permute-done.27
  302.9 437.5 %all-reduce.3.cloned.1.call-done = f32[256,256]{1,0:T(8,128)} async-done(((f32[256,256]{1,0:T(8,128)}), f32[256,256]{1,0:T(8,128)}) %all-reduce.3.cloned.1.call-update) | async-done | bytes 262160 | tf_op jit(solution)/shard_map/psum | solution.py:300
  740.4 1.7 broadcast_multiply_fusion
  (277 shorter events, 32.0 us)
Async XLA Ops:
  7.2 16.1 %copy-start.4 = (f32[1,8,8,128]{3,2,1,0:T(8,128)S(1)}, f32[1,8,8,128]{3,2,1,0:T(8,128)}, u32[]{:S(2)}) copy-start(f32[1,8,8,128]{3,2,1,0:T(8,128)} %param.21) | copy-start | bytes 98308
  7.2 733.2 %all-reduce.3.cloned.1.call-start = ((), (), s32[]{:S(2)}) async-start(), calls=%async_computation | async-start | bytes 524288 | tf_op jit(solution)/shard_map/psum | solution.py:300
  8.0 34.4 %collective-permute-start.12 = (f32[2,2,128]{2,1,0:T(2,128)S(1)}, f32[2,2,128]{2,1,0:T(2,128)S(1)}, u32[]{:S(2)}, u32[]{:S(2)}) collective-permute-start(f32[2,2,128]{2,1,0:T(2,128)S(1)} %get-tuple-element.584), channel_id=1, source_target_pairs={{0,16},{16,32},{32,48},{48,64},{64,80},{80,96},{96,112},{112,128},... | collective-permute-start | bytes 6152 | tf_op jit(solution)/shard_map/ppermute | solution.py:22
  12.5 29.9 %collective-permute-start.13 = (f32[2,2,128]{2,1,0:T(2,128)S(1)}, f32[2,2,128]{2,1,0:T(2,128)S(1)}, u32[]{:S(2)}, u32[]{:S(2)}) collective-permute-start(f32[2,2,128]{2,1,0:T(2,128)S(1)} %get-tuple-element.585), channel_id=1, source_target_pairs={{16,0},{32,16},{48,32},{64,48},{80,64},{96,80},{112,96},{128,112},... | collective-permute-start | bytes 6152 | tf_op jit(solution)/shard_map/ppermute | solution.py:25
  18.1 5.2 copy-start.9
  18.9 6.1 collective-permute-start.1
  20.9 5.0 collective-permute-start
  23.3 0.7 copy-start.10
  23.3 0.7 copy-start.11
  24.0 0.8 copy-start.1
  25.9 2.9 collective-permute-start.3
  27.5 5.3 collective-permute-start.2
  33.1 0.9 copy-start.12
  33.4 0.7 copy-start
  33.4 0.7 copy-start.13
  35.8 6.6 collective-permute-start.5
  40.4 5.0 collective-permute-start.4
  45.5 10.0 %collective-permute-start.7 = (f32[1,8,12,2]{3,2,1,0:T(8,128)S(1)}, f32[1,8,12,2]{3,2,1,0:T(8,128)S(1)}, u32[]{:S(2)}, u32[]{:S(2)}) collective-permute-start(f32[1,8,12,2]{3,2,1,0:T(8,128)S(1)} %get-tuple-element.534), channel_id=1, source_target_pairs={{0,1},{1,2},{2,3},{3,4},{4,5},{5,6},{6,7},{7,8},{8,9},{9,10},{10,1... | collective-permute-start | bytes 2312 | tf_op jit(solution)/shard_map/ppermute | solution.py:22
  48.6 6.9 collective-permute-start.6
  50.0 12.5 %collective-permute-start.14 = (f32[2,12,2]{2,1,0:T(8,128)S(1)}, f32[2,12,2]{2,1,0:T(8,128)S(1)}, u32[]{:S(2)}, u32[]{:S(2)}) collective-permute-start(f32[2,12,2]{2,1,0:T(8,128)S(1)} %get-tuple-element.564), channel_id=1, source_target_pairs={{0,1},{1,2},{2,3},{3,4},{4,5},{5,6},{6,7},{7,8},{8,9},{9,10},{10,1... | collective-permute-start | bytes 584 | tf_op jit(solution)/shard_map/ppermute | solution.py:22
  54.1 8.4 %collective-permute-start.15 = (f32[2,12,2]{2,1,0:T(8,128)S(1)}, f32[2,12,2]{2,1,0:T(8,128)S(1)}, u32[]{:S(2)}, u32[]{:S(2)}) collective-permute-start(f32[2,12,2]{2,1,0:T(8,128)S(1)} %get-tuple-element.565), channel_id=1, source_target_pairs={{1,0},{2,1},{3,2},{4,3},{5,4},{6,5},{7,6},{8,7},{9,8},{10,9},{11,1... | collective-permute-start | bytes 584 | tf_op jit(solution)/shard_map/ppermute | solution.py:25
  57.9 4.7 collective-permute-start.9
  60.6 5.0 collective-permute-start.8
  65.6 6.6 collective-permute-start.11
  70.9 5.2 collective-permute-start.10
  81.2 33.6 %copy-start.5 = (f32[1,12,8,128]{3,2,1,0:T(8,128)}, f32[1,12,8,128]{3,2,1,0:T(8,128)S(1)}, u32[]{:S(2)}) copy-start(f32[1,12,8,128]{3,2,1,0:T(8,128)S(1)} %transpose_reshape_reshape.21) | copy-start | bytes 147460
  81.3 14.3 %collective-permute-start.16 = (f32[1,7,2,128]{3,2,1,0:T(2,128)S(1)}, f32[1,7,2,128]{3,2,1,0:T(2,128)S(1)}, u32[]{:S(2)}, u32[]{:S(2)}) collective-permute-start(f32[1,7,2,128]{3,2,1,0:T(2,128)S(1)} %get-tuple-element.562), channel_id=1, source_target_pairs={{0,16},{16,32},{32,48},{48,64},{64,80},{80,96},{96,112},{112,128},... | collective-permute-start | bytes 21512 | tf_op jit(solution)/shard_map/ppermute | solution.py:22
  92.1 9.6 %collective-permute-start.17 = (f32[1,7,2,128]{3,2,1,0:T(2,128)S(1)}, f32[1,7,2,128]{3,2,1,0:T(2,128)S(1)}, u32[]{:S(2)}, u32[]{:S(2)}) collective-permute-start(f32[1,7,2,128]{3,2,1,0:T(2,128)S(1)} %get-tuple-element.563), channel_id=1, source_target_pairs={{16,0},{32,16},{48,32},{64,48},{80,64},{96,80},{112,96},{128,112},... | collective-permute-start | bytes 21512 | tf_op jit(solution)/shard_map/ppermute | solution.py:25
  101.9 6.1 collective-permute-start.18
  106.5 7.9 %collective-permute-start.19 = (f32[1,7,12,2]{3,2,1,0:T(8,128)S(1)}, f32[1,7,12,2]{3,2,1,0:T(8,128)S(1)}, u32[]{:S(2)}, u32[]{:S(2)}) collective-permute-start(f32[1,7,12,2]{3,2,1,0:T(8,128)S(1)} %get-tuple-element.543), channel_id=1, source_target_pairs={{1,0},{2,1},{3,2},{4,3},{5,4},{6,5},{7,6},{8,7},{9,8},{10,9},{11,1... | collective-permute-start | bytes 2024 | tf_op jit(solution)/shard_map/ppermute | solution.py:25
  119.5 27.8 %copy-start.2 = (f32[1,12,8,128]{3,2,1,0:T(8,128)}, f32[1,12,8,128]{3,2,1,0:T(8,128)S(1)}, u32[]{:S(2)}) copy-start(f32[1,12,8,128]{3,2,1,0:T(8,128)S(1)} %transpose_reshape_reshape.22) | copy-start | bytes 147460
  119.5 0.8 copy-start.6
  119.6 0.8 slice-start.1
  120.5 6.5 collective-permute-start.20
  125.0 10.2 %collective-permute-start.21 = (f32[1,7,2,128]{3,2,1,0:T(2,128)S(1)}, f32[1,7,2,128]{3,2,1,0:T(2,128)S(1)}, u32[]{:S(2)}, u32[]{:S(2)}) collective-permute-start(f32[1,7,2,128]{3,2,1,0:T(2,128)S(1)} %get-tuple-element.561), channel_id=1, source_target_pairs={{16,0},{32,16},{48,32},{64,48},{80,64},{96,80},{112,96},{128,112},... | collective-permute-start | bytes 21512 | tf_op jit(solution)/shard_map/ppermute | solution.py:25
  135.3 7.9 %collective-permute-start.22 = (f32[1,7,12,2]{3,2,1,0:T(8,128)S(1)}, f32[1,7,12,2]{3,2,1,0:T(8,128)S(1)}, u32[]{:S(2)}, u32[]{:S(2)}) collective-permute-start(f32[1,7,12,2]{3,2,1,0:T(8,128)S(1)} %get-tuple-element.540), channel_id=1, source_target_pairs={{0,1},{1,2},{2,3},{3,4},{4,5},{5,6},{6,7},{7,8},{8,9},{9,10},{10,1... | collective-permute-start | bytes 2024 | tf_op jit(solution)/shard_map/ppermute | solution.py:22
  141.3 5.5 collective-permute-start.23
  151.8 0.8 copy-start.3
  151.9 144.8 %copy-start.7 = (f32[1,12,8,128]{3,2,1,0:T(8,128)}, f32[1,12,8,128]{3,2,1,0:T(8,128)S(1)}, u32[]{:S(2)}) copy-start(f32[1,12,8,128]{3,2,1,0:T(8,128)S(1)} %transpose_reshape_reshape.23) | copy-start | bytes 147460
  152.0 0.7 slice-start
  152.9 140.3 %collective-permute-start.24 = (f32[1,7,2,128]{3,2,1,0:T(2,128)S(1)}, f32[1,7,2,128]{3,2,1,0:T(2,128)S(1)}, u32[]{:S(2)}, u32[]{:S(2)}) collective-permute-start(f32[1,7,2,128]{3,2,1,0:T(2,128)S(1)} %get-tuple-element.558), channel_id=1, source_target_pairs={{0,16},{16,32},{32,48},{48,64},{64,80},{80,96},{96,112},{112,128},... | collective-permute-start | bytes 21512 | tf_op jit(solution)/shard_map/ppermute | solution.py:22
  157.2 135.9 %collective-permute-start.25 = (f32[1,7,2,128]{3,2,1,0:T(2,128)S(1)}, f32[1,7,2,128]{3,2,1,0:T(2,128)S(1)}, u32[]{:S(2)}, u32[]{:S(2)}) collective-permute-start(f32[1,7,2,128]{3,2,1,0:T(2,128)S(1)} %get-tuple-element.559), channel_id=1, source_target_pairs={{16,0},{32,16},{48,32},{64,48},{80,64},{96,80},{112,96},{128,112},... | collective-permute-start | bytes 21512 | tf_op jit(solution)/shard_map/ppermute | solution.py:25
  293.2 3.5 collective-permute-start.26
  294.8 5.5 collective-permute-start.27
  300.7 0.7 slice-start.2
  301.4 0.8 copy-start.8
Sparse Core Ops, SparseCore 0:
  293.2 447.0 all-reduce.2
where the time goes:
time: 751 us; the launch traced here: 749 us
  waiting for transfers between devices  480 us (64%)
  blocking collectives  133 us (18%)
  starting transfers between devices  86.4 us (12%)
  matrix products  17.7 us (2%)
  between operations  15.2 us (2%)
  other arithmetic  8.68 us (1%)
  local copies, waits for them, and re-layouts  8.12 us (1%)
    psum x1, waiting for transfers between devices, shards(): lax.psum((local_totals[0], local_totals[1], local_totals[2]), ('warp', 'w...  438 us
    psum x1, blocking collectives, shards(): lax.psum((local_totals[0], local_totals[1], local_totals[2]), ('warp', 'w...  133 us
    ppermute x14, starting transfers between devices, with_halo(): lax.ppermute(lax.slice_in_dim(block, block.shape[dim] - width, None, axis...  59.7 us
    ppermute x14, waiting for transfers between devices, with_halo(): lax.ppermute(lax.slice_in_dim(block, 0, width, axis=dim), axis, backward)  42.4 us
    ppermute x14, starting transfers between devices, with_halo(): lax.ppermute(lax.slice_in_dim(block, 0, width, axis=dim), axis, backward)  26.6 us
  transfers between devices with their start and end apart: 29, of which 11 were waited for; matrix products, arithmetic and copies ran while one was open for 2% of the time, Pallas kernels for 0%

commit v1 on v0

--- a/solution.py
+++ b/solution.py
@@ -1,9 +1,13 @@
 import jax
 import jax.numpy as jnp
 from jax import lax
-from jax.sharding import PartitionSpec as P
+from jax.sharding import Mesh, PartitionSpec as P
 
 SUBSTEPS = 3
+WARP = ("zhi", "x", "core")
+WEFT = ("y", "zlo")
+PLANE = ("x", "core", "y")
+COLUMN = ("zhi", "zlo")
 
 
 time_step = 0.25
@@ -251,11 +255,32 @@
 
 
 def spread_field(current):
-    return with_halo(current, (("warp", 2), ("weft", 3)), 2)
+    return with_halo(current, ((WARP, 2), (WEFT, 3)), 2)
 
 
 def spread_adjoint(carried):
-    return with_halo(carried, (("warp", 2), ("weft", 3)), 2)
+    return with_halo(carried, ((WARP, 2), (WEFT, 3)), 2)
+
+
+def sum_everywhere(totals):
+    first, second, third = totals
+    plane, column = lax.axis_size(PLANE), lax.axis_size(COLUMN)
+    sizes = [second.size, first.size, third.size]
+    flat = jnp.concatenate([second.reshape(-1), first.reshape(-1), third.reshape(-1)])
+    rows = -(-flat.size // (plane * 128))
+    rows = -(-rows // 8) * 8
+    flat = jnp.pad(flat, (0, plane * rows * 128 - flat.size)).reshape(plane, rows, 128)
+    part = jnp.sum(lax.all_to_all(flat, PLANE, 0, 0, tiled=True), axis=0)
+    part = jnp.broadcast_to(part, (column,) + part.shape)
+    part = jnp.sum(lax.all_to_all(part, COLUMN, 0, 0, tiled=True), axis=0)
+    part = jnp.broadcast_to(part, (plane,) + part.shape)
+    flat = lax.all_to_all(part, PLANE, 0, 0, tiled=True).reshape(-1)
+    ends = [sizes[0], sizes[0] + sizes[1], sum(sizes)]
+    return (
+        flat[ends[0] : ends[1]].reshape(first.shape),
+        flat[: ends[0]].reshape(second.shape),
+        flat[ends[1] : ends[2]].reshape(third.shape),
+    )
 
 
 def shards(
@@ -283,7 +308,7 @@
             friction_all(weights, inputs, width), conditions, local_rows, local_columns
         )
         current = advance(padded, stiffness, free, friction)
-    stiff_pad = with_halo(stiffness, (("warp", 1), ("weft", 2)), 2)
+    stiff_pad = with_halo(stiffness, ((WARP, 1), (WEFT, 2)), 2)
     adjoint = final_adjoint
     collected = []
     for substep in reversed(range(SUBSTEPS)):
@@ -297,26 +322,35 @@
             local_totals[1] + later[1],
             local_totals[2] + later[2],
         )
-    totals = lax.psum((local_totals[0], local_totals[1], local_totals[2]), ("warp", "weft"))
-    scale = float(cells * lax.axis_size("warp") * lax.axis_size("weft")) ** (-0.5)
+    totals = sum_everywhere(local_totals)
+    scale = float(cells * lax.axis_size(WARP) * lax.axis_size(WEFT)) ** (-0.5)
     return (current, adjoint, totals[0] * scale, totals[1] * scale, totals[2] * scale)
 
 
+def factors(mesh):
+    warp, weft = mesh.shape["warp"], mesh.shape["weft"]
+    zlo = 4 if weft % 4 == 0 else 1
+    x = 4 if warp % 8 == 0 else 1
+    core = 2 if warp % 2 == 0 else 1
+    return (warp // (x * core), x, core, weft // zlo, zlo)
+
+
 def solution(mesh):
+    fine = Mesh(mesh.devices.reshape(factors(mesh)), WARP + WEFT)
     placed = (
-        P(None, None, "warp", "weft"),
-        P(None, None, "warp", "weft"),
-        P(None, "warp", "weft"),
-        P(None, "warp", "weft"),
-        P("warp", "weft"),
+        P(None, None, WARP, WEFT),
+        P(None, None, WARP, WEFT),
+        P(None, WARP, WEFT),
+        P(None, WARP, WEFT),
+        P(WARP, WEFT),
         P(),
         P(),
         P(),
     )
     return jax.shard_map(
         shards,
-        mesh=mesh,
+        mesh=fine,
         in_specs=placed,
-        out_specs=(P(None, None, "warp", "weft"), P(None, None, "warp", "weft"), P(), P(), P()),
+        out_specs=(P(None, None, WARP, WEFT), P(None, None, WARP, WEFT), P(), P(), P()),
         check_vma=False,
     )

time: 751 us -> 323 us (0.43)
  waiting for transfers between devices: 480 us -> 70.7 us
  blocking collectives: 133 us -> 0 us
  starting transfers between devices: 86.4 us -> 147 us
  matrix products: 17.7 us -> 50.6 us
  local copies, waits for them, and re-layouts: 8.12 us -> 36.1 us
  between operations: 15.2 us -> 1.7 us
    psum x1 -> x0, waiting for transfers between devices: 438 us -> none  [shards(): lax.psum((local_totals[0], local_totals[1], local_totals[2]), ('warp', 'w...]
    psum x1 -> x0, blocking collectives: 133 us -> none  [shards(): lax.psum((local_totals[0], local_totals[1], local_totals[2]), ('warp', 'w...]
    all_to_all x0 -> x3, starting transfers between devices: none -> 55.5 us  [the longest x1 37 us: sum_everywhere(): part = jnp.sum(lax.all_to_all(flat, PLANE, 0, 0, tiled=True), axis=0)]
    all_to_all x0 -> x3, waiting for transfers between devices: none -> 31.4 us  [the longest x1 12.4 us: sum_everywhere(): part = jnp.sum(lax.all_to_all(part, COLUMN, 0, 0, tiled=True), axis=0)]
    slice x0 -> x2, local copies, waits for them, and re-layouts: none -> 26.7 us  [the longest x1 26.5 us: sum_everywhere(): flat[ends[1]:ends[2]].reshape(third.shape)]
    dot_general x24, matrix products: 7.87 us -> 27.1 us  [contract(): lax.dot_general(left, right, (((0,), (0,)), ((), ())), preferred_element_...]
  transfers between devices with their start and end apart: 29 -> 31, of which waited for: 11 -> 13; matrix products, arithmetic and copies ran while one was open for 2% -> 9% of each run, Pallas kernels for 0% -> 0%
where the time goes in v1:
time: 323 us; the launch traced here: 320 us
  starting transfers between devices  147 us (46%)
  waiting for transfers between devices  70.7 us (22%)
  matrix products  50.6 us (16%)
  local copies, waits for them, and re-layouts  36.1 us (11%)
  other arithmetic  13.2 us (4%)
    ppermute x14, starting transfers between devices, with_halo(): lax.ppermute(lax.slice_in_dim(block, block.shape[dim] - width, None, axis...  65.1 us
    ppermute x14, waiting for transfers between devices, with_halo(): lax.ppermute(lax.slice_in_dim(block, 0, width, axis=dim), axis, backward)  39.1 us
    all_to_all x1, starting transfers between devices, sum_everywhere(): part = jnp.sum(lax.all_to_all(flat, PLANE, 0, 0, tiled=True), axis=0)  37 us
    dot_general x24, matrix products, contract(): lax.dot_general(left, right, (((0,), (0,)), ((), ())), preferred_element_...  27.1 us
    ppermute x14, starting transfers between devices, with_halo(): lax.ppermute(lax.slice_in_dim(block, 0, width, axis=dim), axis, backward)  26.6 us
    slice x1, local copies, waits for them, and re-layouts, sum_everywhere(): flat[ends[1]:ends[2]].reshape(third.shape)  26.5 us
    all_to_all x1, waiting for transfers between devices, sum_everywhere(): part = jnp.sum(lax.all_to_all(part, COLUMN, 0, 0, tiled=True), axis=0)  12.4 us
    all_to_all x1, starting transfers between devices, sum_everywhere(): part = jnp.sum(lax.all_to_all(part, COLUMN, 0, 0, tiled=True), axis=0)  10.1 us
  transfers between devices with their start and end apart: 31, of which 13 were waited for; matrix products, arithmetic and copies ran while one was open for 9% of the time, Pallas kernels for 0%

profile of v1, /device:TPU:1, one launch (start us, length us, event | category | flops | bytes accessed | tf_op | source)
XLA Modules:
  0.0 319.9 jit_solution(6923757094677450856)
XLA Ops:
  1.4 4.5 %collective-permute-start.12 = (f32[2,2,128]{2,1,0:T(2,128)S(1)}, f32[2,2,128]{2,1,0:T(2,128)S(1)}, u32[]{:S(2)}, u32[]{:S(2)}) collective-permute-start(f32[2,2,128]{2,1,0:T(2,128)S(1)} %get-tuple-element.592), channel_id=1, source_target_pairs={{0,16},{16,32},{32,48},{48,64},{64,80},{80,96},{96,112},{112,128},... | collective-permute-start | bytes 6152 | tf_op jit(solution)/shard_map/ppermute | solution.py:26
  5.9 5.6 %collective-permute-start.13 = (f32[2,2,128]{2,1,0:T(2,128)S(1)}, f32[2,2,128]{2,1,0:T(2,128)S(1)}, u32[]{:S(2)}, u32[]{:S(2)}) collective-permute-start(f32[2,2,128]{2,1,0:T(2,128)S(1)} %get-tuple-element.593), channel_id=1, source_target_pairs={{16,0},{32,16},{48,32},{64,48},{80,64},{96,80},{112,96},{128,112},... | collective-permute-start | bytes 6152 | tf_op jit(solution)/shard_map/ppermute | solution.py:29
  12.4 1.9 collective-permute-start.1
  14.3 2.4 collective-permute-start
  26.9 4.3 %collective-permute-done.2 = f32[1,8,12,2]{3,2,1,0:T(8,128)S(1)} collective-permute-done((f32[1,8,12,2]{3,2,1,0:T(8,128)S(1)}, f32[1,8,12,2]{3,2,1,0:T(8,128)S(1)}, u32[]{:S(2)}, u32[]{:S(2)}) %collective-permute-start.2) | collective-permute-done | bytes 800 | tf_op jit(solution)/shard_map/ppermute | solution.py:29
  33.2 4.8 %while.81 = (s32[]{:T(128)}, f32[2,2,512]{2,1,0:T(2,128)S(1)}, bf16[2,12,512]{2,1,0:T(8,128)(2,1)S(1)}, bf16[12,256]{1,0:T(8,128)(2,1)}, bf16[256,256]{1,0:T(8,128)(2,1)}, /*index=5*/bf16[256,2]{0,1:T(2,128)(2,1)}, s32[]{:T(128)}) while((s32[]{:T(128)}, f32[2,2,512]{2,1,0:T(2,128)S(1)}, bf16[2,12,512]{2,1,0:T(8,128)(2,1)S(1)}, ...), condition=%wide.region_1.2_spmd, body=%wide.region_0.1_spmd.sunk | while | flops 72089600 | bytes 683101 | solution.py:194
  34.2 1.3 fusion.392
  36.6 1.3 fusion.392
  38.1 4.4 %collective-permute-start.5 = (f32[1,8,2,128]{3,2,1,0:T(2,128)S(1)}, f32[1,8,2,128]{3,2,1,0:T(2,128)S(1)}, u32[]{:S(2)}, u32[]{:S(2)}) collective-permute-start(f32[1,8,2,128]{3,2,1,0:T(2,128)S(1)} %get-tuple-element.562), channel_id=1, source_target_pairs={{0,16},{16,32},{32,48},{48,64},{64,80},{80,96},{96,112},{112,128},... | collective-permute-start | bytes 24584 | tf_op jit(solution)/shard_map/ppermute | solution.py:26
  42.5 1.9 collective-permute-start.4
  44.5 3.0 collective-permute-done.4
  47.6 3.3 %collective-permute-start.7 = (f32[1,8,12,2]{3,2,1,0:T(8,128)S(1)}, f32[1,8,12,2]{3,2,1,0:T(8,128)S(1)}, u32[]{:S(2)}, u32[]{:S(2)}) collective-permute-start(f32[1,8,12,2]{3,2,1,0:T(8,128)S(1)} %get-tuple-element.542), channel_id=1, source_target_pairs={{0,1},{1,2},{2,3},{3,4},{4,5},{5,6},{6,7},{7,8},{8,9},{9,10},{10,1... | collective-permute-start | bytes 2312 | tf_op jit(solution)/shard_map/ppermute | solution.py:26
  52.3 4.2 %collective-permute-start.14 = (f32[2,12,2]{2,1,0:T(8,128)S(1)}, f32[2,12,2]{2,1,0:T(8,128)S(1)}, u32[]{:S(2)}, u32[]{:S(2)}) collective-permute-start(f32[2,12,2]{2,1,0:T(8,128)S(1)} %get-tuple-element.572), channel_id=1, source_target_pairs={{0,1},{1,2},{2,3},{3,4},{4,5},{5,6},{6,7},{7,8},{8,9},{9,10},{10,1... | collective-permute-start | bytes 584 | tf_op jit(solution)/shard_map/ppermute | solution.py:26
  58.5 4.8 %while.82 = (s32[]{:T(128)}, f32[2,2,512]{2,1,0:T(2,128)S(1)}, bf16[2,12,512]{2,1,0:T(8,128)(2,1)S(1)}, bf16[12,256]{1,0:T(8,128)(2,1)}, bf16[256,256]{1,0:T(8,128)(2,1)}, /*index=5*/bf16[256,2]{0,1:T(2,128)(2,1)}, s32[]{:T(128)}) while((s32[]{:T(128)}, f32[2,2,512]{2,1,0:T(2,128)S(1)}, bf16[2,12,512]{2,1,0:T(8,128)(2,1)S(1)}, ...), condition=%wide.region_3.4_spmd, body=%wide.region_2.3_spmd.sunk | while | flops 72089600 | bytes 683101 | solution.py:194
  59.6 1.3 fusion.398
  61.9 1.3 fusion.398
  63.5 3.3 %collective-permute-start.9 = (f32[1,8,2,128]{3,2,1,0:T(2,128)S(1)}, f32[1,8,2,128]{3,2,1,0:T(2,128)S(1)}, u32[]{:S(2)}, u32[]{:S(2)}) collective-permute-start(f32[1,8,2,128]{3,2,1,0:T(2,128)S(1)} %get-tuple-element.560), channel_id=1, source_target_pairs={{0,16},{16,32},{32,48},{48,64},{64,80},{80,96},{96,112},{112,128},... | collective-permute-start | bytes 24584 | tf_op jit(solution)/shard_map/ppermute | solution.py:26
  66.7 1.9 collective-permute-start.8
  68.8 2.9 collective-permute-done.8
  71.8 4.4 %collective-permute-start.11 = (f32[1,8,12,2]{3,2,1,0:T(8,128)S(1)}, f32[1,8,12,2]{3,2,1,0:T(8,128)S(1)}, u32[]{:S(2)}, u32[]{:S(2)}) collective-permute-start(f32[1,8,12,2]{3,2,1,0:T(8,128)S(1)} %get-tuple-element.540), channel_id=1, source_target_pairs={{0,1},{1,2},{2,3},{3,4},{4,5},{5,6},{6,7},{7,8},{8,9},{9,10},{10,1... | collective-permute-start | bytes 2312 | tf_op jit(solution)/shard_map/ppermute | solution.py:26
  77.6 3.9 %collective-permute-done.10 = f32[1,8,12,2]{3,2,1,0:T(8,128)S(1)} collective-permute-done((f32[1,8,12,2]{3,2,1,0:T(8,128)S(1)}, f32[1,8,12,2]{3,2,1,0:T(8,128)S(1)}, u32[]{:S(2)}, u32[]{:S(2)}) %collective-permute-start.10) | collective-permute-done | bytes 800 | tf_op jit(solution)/shard_map/ppermute | solution.py:29
  82.2 12.2 %while.84 = (s32[]{:T(128)}, f32[12,256]{1,0:T(8,128)S(1)}, f32[256,256]{1,0:T(8,128)S(1)}, f32[256,2]{0,1:T(2,128)S(1)}, f32[2,12,512]{2,1,0:T(8,128)S(1)}, /*i...) while((s32[]{:T(128)}, f32[12,256]{1,0:T(8,128)S(1)}, ...), condition=%wide.region_7.8_spmd.clone, body=%wide.region_6.7_spmd.clone.sunk | while | flops 216275968 | bytes 6145181 | solution.py:204
  94.5 6.7 %collective-permute-start.16 = (f32[1,7,2,128]{3,2,1,0:T(2,128)S(1)}, f32[1,7,2,128]{3,2,1,0:T(2,128)S(1)}, u32[]{:S(2)}, u32[]{:S(2)}) collective-permute-start(f32[1,7,2,128]{3,2,1,0:T(2,128)S(1)} %get-tuple-element.570), channel_id=1, source_target_pairs={{0,16},{16,32},{32,48},{48,64},{64,80},{80,96},{96,112},{112,128},... | collective-permute-start | bytes 21512 | tf_op jit(solution)/shard_map/ppermute | solution.py:26
  101.2 1.9 collective-permute-start.17
  103.2 4.8 %while.83 = (s32[]{:T(128)}, f32[2,2,512]{2,1,0:T(2,128)S(1)}, bf16[2,12,512]{2,1,0:T(8,128)(2,1)S(1)}, bf16[12,256]{1,0:T(8,128)(2,1)}, bf16[256,256]{1,0:T(8,128)(2,1)}, /*index=5*/bf16[256,2]{0,1:T(2,128)(2,1)}, s32[]{:T(128)}) while((s32[]{:T(128)}, f32[2,2,512]{2,1,0:T(2,128)S(1)}, bf16[2,12,512]{2,1,0:T(8,128)(2,1)S(1)}, ...), condition=%wide.region_5.6_spmd, body=%wide.region_4.5_spmd.sunk | while | flops 72089600 | bytes 683101 | solution.py:194
  104.2 1.3 fusion.404
  106.6 1.3 fusion.404
  107.9 2.9 collective-permute-done.17
  110.9 4.6 %collective-permute-start.18 = (f32[1,7,12,2]{3,2,1,0:T(8,128)S(1)}, f32[1,7,12,2]{3,2,1,0:T(8,128)S(1)}, u32[]{:S(2)}, u32[]{:S(2)}) collective-permute-start(f32[1,7,12,2]{3,2,1,0:T(8,128)S(1)} %get-tuple-element.550), channel_id=1, source_target_pairs={{0,1},{1,2},{2,3},{3,4},{4,5},{5,6},{6,7},{7,8},{8,9},{9,10},{10,1... | collective-permute-start | bytes 2024 | tf_op jit(solution)/shard_map/ppermute | solution.py:26
  117.0 6.5 %collective-permute-done.19 = f32[1,7,12,2]{3,2,1,0:T(8,128)S(1)} collective-permute-done((f32[1,7,12,2]{3,2,1,0:T(8,128)S(1)}, f32[1,7,12,2]{3,2,1,0:T(8,128)S(1)}, u32[]{:S(2)}, u32[]{:S(2)}) %collective-permute-start.19) | collective-permute-done | bytes 704 | tf_op jit(solution)/shard_map/ppermute | solution.py:29
  124.0 12.2 %while.85 = (s32[]{:T(128)}, f32[12,256]{1,0:T(8,128)S(1)}, f32[256,256]{1,0:T(8,128)S(1)}, f32[256,2]{0,1:T(2,128)S(1)}, f32[2,12,512]{2,1,0:T(8,128)S(1)}, /*i...) while((s32[]{:T(128)}, f32[12,256]{1,0:T(8,128)S(1)}, ...), condition=%wide.region_9.10_spmd.clone, body=%wide.region_8.9_spmd.clone.sunk | while | flops 216275968 | bytes 6145181 | solution.py:204
  136.5 9.4 %collective-permute-start.20 = (f32[1,7,2,128]{3,2,1,0:T(2,128)S(1)}, f32[1,7,2,128]{3,2,1,0:T(2,128)S(1)}, u32[]{:S(2)}, u32[]{:S(2)}) collective-permute-start(f32[1,7,2,128]{3,2,1,0:T(2,128)S(1)} %get-tuple-element.568), channel_id=1, source_target_pairs={{0,16},{16,32},{32,48},{48,64},{64,80},{80,96},{96,112},{112,128},... | collective-permute-start | bytes 21512 | tf_op jit(solution)/shard_map/ppermute | solution.py:26
  145.9 1.9 collective-permute-start.21
  147.9 8.2 %collective-permute-done.21 = f32[1,7,2,128]{3,2,1,0:T(2,128)S(1)} collective-permute-done((f32[1,7,2,128]{3,2,1,0:T(2,128)S(1)}, f32[1,7,2,128]{3,2,1,0:T(2,128)S(1)}, u32[]{:S(2)}, u32[]{:S(2)}) %collective-permute-start.21) | collective-permute-done | bytes 7200 | tf_op jit(solution)/shard_map/ppermute | solution.py:29
  156.1 6.1 %collective-permute-start.22 = (f32[1,7,12,2]{3,2,1,0:T(8,128)S(1)}, f32[1,7,12,2]{3,2,1,0:T(8,128)S(1)}, u32[]{:S(2)}, u32[]{:S(2)}) collective-permute-start(f32[1,7,12,2]{3,2,1,0:T(8,128)S(1)} %get-tuple-element.548), channel_id=1, source_target_pairs={{0,1},{1,2},{2,3},{3,4},{4,5},{5,6},{6,7},{7,8},{8,9},{9,10},{10,1... | collective-permute-start | bytes 2024 | tf_op jit(solution)/shard_map/ppermute | solution.py:26
  164.1 3.6 %collective-permute-done.23 = f32[1,7,12,2]{3,2,1,0:T(8,128)S(1)} collective-permute-done((f32[1,7,12,2]{3,2,1,0:T(8,128)S(1)}, f32[1,7,12,2]{3,2,1,0:T(8,128)S(1)}, u32[]{:S(2)}, u32[]{:S(2)}) %collective-permute-start.23) | collective-permute-done | bytes 704 | tf_op jit(solution)/shard_map/ppermute | solution.py:29
  168.2 12.2 %while.86 = (s32[]{:T(128)}, f32[12,256]{1,0:T(8,128)S(1)}, f32[256,256]{1,0:T(8,128)S(1)}, f32[256,2]{0,1:T(2,128)S(1)}, f32[2,12,512]{2,1,0:T(8,128)S(1)}, /*i...) while((s32[]{:T(128)}, f32[12,256]{1,0:T(8,128)S(1)}, ...), condition=%wide.region_11.12_spmd.clone, body=%wide.region_10.11_spmd.clone.sunk | while | flops 216275968 | bytes 6145181 | solution.py:204
  180.8 7.1 %collective-permute-start.24 = (f32[1,7,2,128]{3,2,1,0:T(2,128)S(1)}, f32[1,7,2,128]{3,2,1,0:T(2,128)S(1)}, u32[]{:S(2)}, u32[]{:S(2)}) collective-permute-start(f32[1,7,2,128]{3,2,1,0:T(2,128)S(1)} %get-tuple-element.566), channel_id=1, source_target_pairs={{0,16},{16,32},{32,48},{48,64},{64,80},{80,96},{96,112},{112,128},... | collective-permute-start | bytes 21512 | tf_op jit(solution)/shard_map/ppermute | solution.py:26
  187.9 1.9 collective-permute-start.25
  190.4 3.9 %collective-permute-done.25 = f32[1,7,2,128]{3,2,1,0:T(2,128)S(1)} collective-permute-done((f32[1,7,2,128]{3,2,1,0:T(2,128)S(1)}, f32[1,7,2,128]{3,2,1,0:T(2,128)S(1)}, u32[]{:S(2)}, u32[]{:S(2)}) %collective-permute-start.25) | collective-permute-done | bytes 7200 | tf_op jit(solution)/shard_map/ppermute | solution.py:29
  194.3 4.0 %collective-permute-start.26 = (f32[1,7,12,2]{3,2,1,0:T(8,128)S(1)}, f32[1,7,12,2]{3,2,1,0:T(8,128)S(1)}, u32[]{:S(2)}, u32[]{:S(2)}) collective-permute-start(f32[1,7,12,2]{3,2,1,0:T(8,128)S(1)} %get-tuple-element.546), channel_id=1, source_target_pairs={{0,1},{1,2},{2,3},{3,4},{4,5},{5,6},{6,7},{7,8},{8,9},{9,10},{10,1... | collective-permute-start | bytes 2024 | tf_op jit(solution)/shard_map/ppermute | solution.py:26
  200.5 37.0 %all-to-all-start = ((f32[32,24,128]{2,1,0:T(8,128)}), f32[32,24,128]{2,1,0:T(8,128)S(1)}, u32[]{:S(2)}, u32[]{:S(2)}) async-start(f32[32,24,128]{2,1,0:T(8,128)} %bitcast.88), calls=%async_computation | async-start | bytes 786432 | tf_op jit(solution)/shard_map/all_to_all | solution.py:273
  237.8 9.8 %all-to-all-done = f32[32,24,128]{2,1,0:T(8,128)S(1)} async-done(((f32[32,24,128]{2,1,0:T(8,128)}), f32[32,24,128]{2,1,0:T(8,128)S(1)}, u32[]{:S(2)}, u32[]{:S(2)}) %all-to-all-start) | async-done | bytes 393248 | tf_op jit(solution)/shard_map/all_to_all | solution.py:273
  248.3 10.1 %all-to-all-start.1 = ((f32[16,24,128]{2,1,0:T(8,128)}), f32[16,24,128]{2,1,0:T(8,128)S(1)}, u32[]{:S(2)}, u32[]{:S(2)}) async-start(f32[16,24,128]{2,1,0:T(8,128)} %broadcast_in_dim.35), calls=%async_computation.1 | async-start | bytes 393216 | tf_op jit(solution)/shard_map/all_to_all | solution.py:275
  258.6 12.4 %all-to-all-done.1 = f32[16,24,128]{2,1,0:T(8,128)S(1)} async-done(((f32[16,24,128]{2,1,0:T(8,128)}), f32[16,24,128]{2,1,0:T(8,128)S(1)}, u32[]{:S(2)}, u32[]{:S(2)}) %all-to-all-start.1) | async-done | bytes 196640 | tf_op jit(solution)/shard_map/all_to_all | solution.py:275
  271.8 8.4 %all-to-all-start.2 = ((f32[32,24,128]{2,1,0:T(8,128)}), f32[32,24,128]{2,1,0:T(8,128)S(1)}, u32[]{:S(2)}, u32[]{:S(2)}) async-start(f32[32,24,128]{2,1,0:T(8,128)} %broadcast_in_dim.36), calls=%async_computation.2 | async-start | bytes 786432 | tf_op jit(solution)/shard_map/all_to_all | solution.py:277
  281.0 9.3 %all-to-all-done.2 = f32[32,24,128]{2,1,0:T(8,128)S(1)} async-done(((f32[32,24,128]{2,1,0:T(8,128)}), f32[32,24,128]{2,1,0:T(8,128)S(1)}, u32[]{:S(2)}, u32[]{:S(2)}) %all-to-all-start.2) | async-done | bytes 393248 | tf_op jit(solution)/shard_map/all_to_all | solution.py:277
  291.7 26.5 %slice.1173 = f32[49152,2]{1,0:T(8,128)} reshape(f32[32,24,128]{2,1,0:T(8,128)S(1)} %all-to-all-done.2) | data formatting | bytes 786432 | tf_op jit(solution)/shard_map/slice | solution.py:282
  (266 shorter events, 75.8 us)
Async XLA Ops:
  0.6 43.8 %copy-start.2 = (f32[2,8,128]{2,1,0:T(8,128)S(1)}, f32[2,8,128]{2,1,0:T(8,128)}, u32[]{:S(2)}) copy-start(f32[2,8,128]{2,1,0:T(8,128)} %param.22) | copy-start | bytes 24580
  0.6 37.3 %copy-start = (f32[1,8,8,128]{3,2,1,0:T(8,128)S(1)}, f32[1,8,8,128]{3,2,1,0:T(8,128)}, u32[]{:S(2)}) copy-start(f32[1,8,8,128]{3,2,1,0:T(8,128)} %param.20) | copy-start | bytes 98308
  1.4 43.0 %collective-permute-start.12 = (f32[2,2,128]{2,1,0:T(2,128)S(1)}, f32[2,2,128]{2,1,0:T(2,128)S(1)}, u32[]{:S(2)}, u32[]{:S(2)}) collective-permute-start(f32[2,2,128]{2,1,0:T(2,128)S(1)} %get-tuple-element.592), channel_id=1, source_target_pairs={{0,16},{16,32},{32,48},{48,64},{64,80},{80,96},{96,112},{112,128},... | collective-permute-start | bytes 6152 | tf_op jit(solution)/shard_map/ppermute | solution.py:26
  5.9 38.5 %collective-permute-start.13 = (f32[2,2,128]{2,1,0:T(2,128)S(1)}, f32[2,2,128]{2,1,0:T(2,128)S(1)}, u32[]{:S(2)}, u32[]{:S(2)}) collective-permute-start(f32[2,2,128]{2,1,0:T(2,128)S(1)} %get-tuple-element.593), channel_id=1, source_target_pairs={{16,0},{32,16},{48,32},{64,48},{80,64},{96,80},{112,96},{128,112},... | collective-permute-start | bytes 6152 | tf_op jit(solution)/shard_map/ppermute | solution.py:29
  12.4 10.9 %collective-permute-start.1 = (f32[1,8,2,128]{3,2,1,0:T(2,128)S(1)}, f32[1,8,2,128]{3,2,1,0:T(2,128)S(1)}, u32[]{:S(2)}, u32[]{:S(2)}) collective-permute-start(f32[1,8,2,128]{3,2,1,0:T(2,128)S(1)} %get-tuple-element.564), channel_id=1, source_target_pairs={{0,16},{16,32},{32,48},{48,64},{64,80},{80,96},{96,112},{112,128},... | collective-permute-start | bytes 24584 | tf_op jit(solution)/shard_map/ppermute | solution.py:26
  14.3 9.0 %collective-permute-start = (f32[1,8,2,128]{3,2,1,0:T(2,128)S(1)}, f32[1,8,2,128]{3,2,1,0:T(2,128)S(1)}, u32[]{:S(2)}, u32[]{:S(2)}) collective-permute-start(f32[1,8,2,128]{3,2,1,0:T(2,128)S(1)} %get-tuple-element.565), channel_id=1, source_target_pairs={{16,0},{32,16},{48,32},{64,48},{80,64},{96,80},{112,96},{128,112},... | collective-permute-start | bytes 24584 | tf_op jit(solution)/shard_map/ppermute | solution.py:29
  24.2 2.8 collective-permute-start.3
  25.5 5.7 %collective-permute-start.2 = (f32[1,8,12,2]{3,2,1,0:T(8,128)S(1)}, f32[1,8,12,2]{3,2,1,0:T(8,128)S(1)}, u32[]{:S(2)}, u32[]{:S(2)}) collective-permute-start(f32[1,8,12,2]{3,2,1,0:T(8,128)S(1)} %get-tuple-element.545), channel_id=1, source_target_pairs={{1,0},{2,1},{3,2},{4,3},{5,4},{6,5},{7,6},{8,7},{9,8},{10,9},{11,1... | collective-permute-start | bytes 2312 | tf_op jit(solution)/shard_map/ppermute | solution.py:29
  38.1 6.4 %collective-permute-start.5 = (f32[1,8,2,128]{3,2,1,0:T(2,128)S(1)}, f32[1,8,2,128]{3,2,1,0:T(2,128)S(1)}, u32[]{:S(2)}, u32[]{:S(2)}) collective-permute-start(f32[1,8,2,128]{3,2,1,0:T(2,128)S(1)} %get-tuple-element.562), channel_id=1, source_target_pairs={{0,16},{16,32},{32,48},{48,64},{64,80},{80,96},{96,112},{112,128},... | collective-permute-start | bytes 24584 | tf_op jit(solution)/shard_map/ppermute | solution.py:26
  42.5 5.0 %collective-permute-start.4 = (f32[1,8,2,128]{3,2,1,0:T(2,128)S(1)}, f32[1,8,2,128]{3,2,1,0:T(2,128)S(1)}, u32[]{:S(2)}, u32[]{:S(2)}) collective-permute-start(f32[1,8,2,128]{3,2,1,0:T(2,128)S(1)} %get-tuple-element.563), channel_id=1, source_target_pairs={{16,0},{32,16},{48,32},{64,48},{80,64},{96,80},{112,96},{128,112},... | collective-permute-start | bytes 24584 | tf_op jit(solution)/shard_map/ppermute | solution.py:29
  47.6 10.3 %collective-permute-start.7 = (f32[1,8,12,2]{3,2,1,0:T(8,128)S(1)}, f32[1,8,12,2]{3,2,1,0:T(8,128)S(1)}, u32[]{:S(2)}, u32[]{:S(2)}) collective-permute-start(f32[1,8,12,2]{3,2,1,0:T(8,128)S(1)} %get-tuple-element.542), channel_id=1, source_target_pairs={{0,1},{1,2},{2,3},{3,4},{4,5},{5,6},{6,7},{7,8},{8,9},{9,10},{10,1... | collective-permute-start | bytes 2312 | tf_op jit(solution)/shard_map/ppermute | solution.py:26
  50.9 6.9 %collective-permute-start.6 = (f32[1,8,12,2]{3,2,1,0:T(8,128)S(1)}, f32[1,8,12,2]{3,2,1,0:T(8,128)S(1)}, u32[]{:S(2)}, u32[]{:S(2)}) collective-permute-start(f32[1,8,12,2]{3,2,1,0:T(8,128)S(1)} %get-tuple-element.543), channel_id=1, source_target_pairs={{1,0},{2,1},{3,2},{4,3},{5,4},{6,5},{7,6},{8,7},{9,8},{10,9},{11,1... | collective-permute-start | bytes 2312 | tf_op jit(solution)/shard_map/ppermute | solution.py:29
  52.3 16.4 %collective-permute-start.14 = (f32[2,12,2]{2,1,0:T(8,128)S(1)}, f32[2,12,2]{2,1,0:T(8,128)S(1)}, u32[]{:S(2)}, u32[]{:S(2)}) collective-permute-start(f32[2,12,2]{2,1,0:T(8,128)S(1)} %get-tuple-element.572), channel_id=1, source_target_pairs={{0,1},{1,2},{2,3},{3,4},{4,5},{5,6},{6,7},{7,8},{8,9},{9,10},{10,1... | collective-permute-start | bytes 584 | tf_op jit(solution)/shard_map/ppermute | solution.py:26
  56.5 12.2 %collective-permute-start.15 = (f32[2,12,2]{2,1,0:T(8,128)S(1)}, f32[2,12,2]{2,1,0:T(8,128)S(1)}, u32[]{:S(2)}, u32[]{:S(2)}) collective-permute-start(f32[2,12,2]{2,1,0:T(8,128)S(1)} %get-tuple-element.573), channel_id=1, source_target_pairs={{1,0},{2,1},{3,2},{4,3},{5,4},{6,5},{7,6},{8,7},{9,8},{10,9},{11,1... | collective-permute-start | bytes 584 | tf_op jit(solution)/shard_map/ppermute | solution.py:29
  63.5 5.3 %collective-permute-start.9 = (f32[1,8,2,128]{3,2,1,0:T(2,128)S(1)}, f32[1,8,2,128]{3,2,1,0:T(2,128)S(1)}, u32[]{:S(2)}, u32[]{:S(2)}) collective-permute-start(f32[1,8,2,128]{3,2,1,0:T(2,128)S(1)} %get-tuple-element.560), channel_id=1, source_target_pairs={{0,16},{16,32},{32,48},{48,64},{64,80},{80,96},{96,112},{112,128},... | collective-permute-start | bytes 24584 | tf_op jit(solution)/shard_map/ppermute | solution.py:26
  66.7 5.0 %collective-permute-start.8 = (f32[1,8,2,128]{3,2,1,0:T(2,128)S(1)}, f32[1,8,2,128]{3,2,1,0:T(2,128)S(1)}, u32[]{:S(2)}, u32[]{:S(2)}) collective-permute-start(f32[1,8,2,128]{3,2,1,0:T(2,128)S(1)} %get-tuple-element.561), channel_id=1, source_target_pairs={{16,0},{32,16},{48,32},{64,48},{80,64},{96,80},{112,96},{128,112},... | collective-permute-start | bytes 24584 | tf_op jit(solution)/shard_map/ppermute | solution.py:29
  71.8 5.8 %collective-permute-start.11 = (f32[1,8,12,2]{3,2,1,0:T(8,128)S(1)}, f32[1,8,12,2]{3,2,1,0:T(8,128)S(1)}, u32[]{:S(2)}, u32[]{:S(2)}) collective-permute-start(f32[1,8,12,2]{3,2,1,0:T(8,128)S(1)} %get-tuple-element.540), channel_id=1, source_target_pairs={{0,1},{1,2},{2,3},{3,4},{4,5},{5,6},{6,7},{7,8},{8,9},{9,10},{10,1... | collective-permute-start | bytes 2312 | tf_op jit(solution)/shard_map/ppermute | solution.py:26
  76.2 5.3 %collective-permute-start.10 = (f32[1,8,12,2]{3,2,1,0:T(8,128)S(1)}, f32[1,8,12,2]{3,2,1,0:T(8,128)S(1)}, u32[]{:S(2)}, u32[]{:S(2)}) collective-permute-start(f32[1,8,12,2]{3,2,1,0:T(8,128)S(1)} %get-tuple-element.541), channel_id=1, source_target_pairs={{1,0},{2,1},{3,2},{4,3},{5,4},{6,5},{7,6},{8,7},{9,8},{10,9},{11,1... | collective-permute-start | bytes 2312 | tf_op jit(solution)/shard_map/ppermute | solution.py:29
  82.2 12.3 %copy-start.1 = (f32[1,8,8,128]{3,2,1,0:T(8,128)S(1)}, f32[1,8,8,128]{3,2,1,0:T(8,128)}, u32[]{:S(2)}) copy-start(f32[1,8,8,128]{3,2,1,0:T(8,128)} %param.21) | copy-start | bytes 98308
  94.5 13.4 %collective-permute-start.16 = (f32[1,7,2,128]{3,2,1,0:T(2,128)S(1)}, f32[1,7,2,128]{3,2,1,0:T(2,128)S(1)}, u32[]{:S(2)}, u32[]{:S(2)}) collective-permute-start(f32[1,7,2,128]{3,2,1,0:T(2,128)S(1)} %get-tuple-element.570), channel_id=1, source_target_pairs={{0,16},{16,32},{32,48},{48,64},{64,80},{80,96},{96,112},{112,128},... | collective-permute-start | bytes 21512 | tf_op jit(solution)/shard_map/ppermute | solution.py:26
  101.2 9.6 %collective-permute-start.17 = (f32[1,7,2,128]{3,2,1,0:T(2,128)S(1)}, f32[1,7,2,128]{3,2,1,0:T(2,128)S(1)}, u32[]{:S(2)}, u32[]{:S(2)}) collective-permute-start(f32[1,7,2,128]{3,2,1,0:T(2,128)S(1)} %get-tuple-element.571), channel_id=1, source_target_pairs={{16,0},{32,16},{48,32},{64,48},{80,64},{96,80},{112,96},{128,112},... | collective-permute-start | bytes 21512 | tf_op jit(solution)/shard_map/ppermute | solution.py:29
  110.9 6.1 %collective-permute-start.18 = (f32[1,7,12,2]{3,2,1,0:T(8,128)S(1)}, f32[1,7,12,2]{3,2,1,0:T(8,128)S(1)}, u32[]{:S(2)}, u32[]{:S(2)}) collective-permute-start(f32[1,7,12,2]{3,2,1,0:T(8,128)S(1)} %get-tuple-element.550), channel_id=1, source_target_pairs={{0,1},{1,2},{2,3},{3,4},{4,5},{5,6},{6,7},{7,8},{8,9},{9,10},{10,1... | collective-permute-start | bytes 2024 | tf_op jit(solution)/shard_map/ppermute | solution.py:26
  115.6 7.9 %collective-permute-start.19 = (f32[1,7,12,2]{3,2,1,0:T(8,128)S(1)}, f32[1,7,12,2]{3,2,1,0:T(8,128)S(1)}, u32[]{:S(2)}, u32[]{:S(2)}) collective-permute-start(f32[1,7,12,2]{3,2,1,0:T(8,128)S(1)} %get-tuple-element.551), channel_id=1, source_target_pairs={{1,0},{2,1},{3,2},{4,3},{5,4},{6,5},{7,6},{8,7},{9,8},{10,9},{11,1... | collective-permute-start | bytes 2024 | tf_op jit(solution)/shard_map/ppermute | solution.py:29
  136.5 11.4 %collective-permute-start.20 = (f32[1,7,2,128]{3,2,1,0:T(2,128)S(1)}, f32[1,7,2,128]{3,2,1,0:T(2,128)S(1)}, u32[]{:S(2)}, u32[]{:S(2)}) collective-permute-start(f32[1,7,2,128]{3,2,1,0:T(2,128)S(1)} %get-tuple-element.568), channel_id=1, source_target_pairs={{0,16},{16,32},{32,48},{48,64},{64,80},{80,96},{96,112},{112,128},... | collective-permute-start | bytes 21512 | tf_op jit(solution)/shard_map/ppermute | solution.py:26
  145.9 10.1 %collective-permute-start.21 = (f32[1,7,2,128]{3,2,1,0:T(2,128)S(1)}, f32[1,7,2,128]{3,2,1,0:T(2,128)S(1)}, u32[]{:S(2)}, u32[]{:S(2)}) collective-permute-start(f32[1,7,2,128]{3,2,1,0:T(2,128)S(1)} %get-tuple-element.569), channel_id=1, source_target_pairs={{16,0},{32,16},{48,32},{64,48},{80,64},{96,80},{112,96},{128,112},... | collective-permute-start | bytes 21512 | tf_op jit(solution)/shard_map/ppermute | solution.py:29
  156.1 8.0 %collective-permute-start.22 = (f32[1,7,12,2]{3,2,1,0:T(8,128)S(1)}, f32[1,7,12,2]{3,2,1,0:T(8,128)S(1)}, u32[]{:S(2)}, u32[]{:S(2)}) collective-permute-start(f32[1,7,12,2]{3,2,1,0:T(8,128)S(1)} %get-tuple-element.548), channel_id=1, source_target_pairs={{0,1},{1,2},{2,3},{3,4},{4,5},{5,6},{6,7},{7,8},{8,9},{9,10},{10,1... | collective-permute-start | bytes 2024 | tf_op jit(solution)/shard_map/ppermute | solution.py:26
  162.2 5.5 %collective-permute-start.23 = (f32[1,7,12,2]{3,2,1,0:T(8,128)S(1)}, f32[1,7,12,2]{3,2,1,0:T(8,128)S(1)}, u32[]{:S(2)}, u32[]{:S(2)}) collective-permute-start(f32[1,7,12,2]{3,2,1,0:T(8,128)S(1)} %get-tuple-element.549), channel_id=1, source_target_pairs={{1,0},{2,1},{3,2},{4,3},{5,4},{6,5},{7,6},{8,7},{9,8},{10,9},{11,1... | collective-permute-start | bytes 2024 | tf_op jit(solution)/shard_map/ppermute | solution.py:29
  180.8 9.6 %collective-permute-start.24 = (f32[1,7,2,128]{3,2,1,0:T(2,128)S(1)}, f32[1,7,2,128]{3,2,1,0:T(2,128)S(1)}, u32[]{:S(2)}, u32[]{:S(2)}) collective-permute-start(f32[1,7,2,128]{3,2,1,0:T(2,128)S(1)} %get-tuple-element.566), channel_id=1, source_target_pairs={{0,16},{16,32},{32,48},{48,64},{64,80},{80,96},{96,112},{112,128},... | collective-permute-start | bytes 21512 | tf_op jit(solution)/shard_map/ppermute | solution.py:26
  187.9 6.3 %collective-permute-start.25 = (f32[1,7,2,128]{3,2,1,0:T(2,128)S(1)}, f32[1,7,2,128]{3,2,1,0:T(2,128)S(1)}, u32[]{:S(2)}, u32[]{:S(2)}) collective-permute-start(f32[1,7,2,128]{3,2,1,0:T(2,128)S(1)} %get-tuple-element.567), channel_id=1, source_target_pairs={{16,0},{32,16},{48,32},{64,48},{80,64},{96,80},{112,96},{128,112},... | collective-permute-start | bytes 21512 | tf_op jit(solution)/shard_map/ppermute | solution.py:29
  194.3 43.2 %collective-permute-start.26 = (f32[1,7,12,2]{3,2,1,0:T(8,128)S(1)}, f32[1,7,12,2]{3,2,1,0:T(8,128)S(1)}, u32[]{:S(2)}, u32[]{:S(2)}) collective-permute-start(f32[1,7,12,2]{3,2,1,0:T(8,128)S(1)} %get-tuple-element.546), channel_id=1, source_target_pairs={{0,1},{1,2},{2,3},{3,4},{4,5},{5,6},{6,7},{7,8},{8,9},{9,10},{10,1... | collective-permute-start | bytes 2024 | tf_op jit(solution)/shard_map/ppermute | solution.py:26
  198.4 39.2 %collective-permute-start.27 = (f32[1,7,12,2]{3,2,1,0:T(8,128)S(1)}, f32[1,7,12,2]{3,2,1,0:T(8,128)S(1)}, u32[]{:S(2)}, u32[]{:S(2)}) collective-permute-start(f32[1,7,12,2]{3,2,1,0:T(8,128)S(1)} %get-tuple-element.547), channel_id=1, source_target_pairs={{1,0},{2,1},{3,2},{4,3},{5,4},{6,5},{7,6},{8,7},{9,8},{10,9},{11,1... | collective-permute-start | bytes 2024 | tf_op jit(solution)/shard_map/ppermute | solution.py:29
  200.5 47.1 %all-to-all-start = ((f32[32,24,128]{2,1,0:T(8,128)}), f32[32,24,128]{2,1,0:T(8,128)S(1)}, u32[]{:S(2)}, u32[]{:S(2)}) async-start(f32[32,24,128]{2,1,0:T(8,128)} %bitcast.88), calls=%async_computation | async-start | bytes 786432 | tf_op jit(solution)/shard_map/all_to_all | solution.py:273
  248.3 22.7 %all-to-all-start.1 = ((f32[16,24,128]{2,1,0:T(8,128)}), f32[16,24,128]{2,1,0:T(8,128)S(1)}, u32[]{:S(2)}, u32[]{:S(2)}) async-start(f32[16,24,128]{2,1,0:T(8,128)} %broadcast_in_dim.35), calls=%async_computation.1 | async-start | bytes 393216 | tf_op jit(solution)/shard_map/all_to_all | solution.py:275
  271.8 18.5 %all-to-all-start.2 = ((f32[32,24,128]{2,1,0:T(8,128)}), f32[32,24,128]{2,1,0:T(8,128)S(1)}, u32[]{:S(2)}, u32[]{:S(2)}) async-start(f32[32,24,128]{2,1,0:T(8,128)} %broadcast_in_dim.36), calls=%async_computation.2 | async-start | bytes 786432 | tf_op jit(solution)/shard_map/all_to_all | solution.py:277

commit v2 on v1

v2 whole, which is shorter than its diff:
```python
import functools

import jax
import jax.numpy as jnp
from jax import lax
from jax.experimental import pallas as pl
from jax.experimental.pallas import tpu as pltpu
from jax.sharding import Mesh, PartitionSpec as P

WARP = ("zhi", "x", "core")
WEFT = ("y", "zlo")
PLANE = ("x", "core", "y")
COLUMN = ("zhi", "zlo")

DT = 0.25
DAMP = 0.9
KB = 0.25
KC = 0.5
KS = 0.5
GRAV = 0.3

TILE_ROWS = 8
LANES = 128
REACH = 10
FIRST = REACH
ALL_ROWS = TILE_ROWS + 2 * REACH
HID = 256
CHUNK = 256
OWN = TILE_ROWS * LANES
F32 = jnp.float32
BF16 = jnp.bfloat16


def span(radius):
    return range(FIRST - radius, FIRST + TILE_ROWS + radius)


def distance(row):
    return max(FIRST - row, row - (FIRST + TILE_ROWS - 1), 0)


def ring(e):
    return [FIRST - e, FIRST + TILE_ROWS - 1 + e]


class Plan:
    def __init__(self, reach, back):
        self.reach, self.back = reach, back
        own = list(range(FIRST, FIRST + TILE_ROWS))
        order = own + [r for e in range(1, back + 1) for r in ring(e)]
        near = len(order)
        order = order + [None] + [r for e in range(back + 1, reach + 1) for r in ring(e)]
        self.tile = {r: t for t, r in enumerate(order) if r is not None}
        self.forward, self.backward = {}, {}
        at = {near: 0, len(order): 0}

        def put(table, row, tile, width):
            table[row] = (tile, at[tile], width)
            at[tile] += 2 * width

        for r in own:
            put(self.forward, r, near, reach)
            self.backward[r] = self.forward[r]
        for e in range(1, reach):
            width, need = reach - e, back - e
            for r in ring(e):
                if need > 0 and at[near] + 2 * width <= LANES and (e == 1 or reach == back):
                    put(self.forward, r, near, width)
                    self.backward[r] = self.forward[r]
                else:
                    put(self.forward, r, len(order), width)
                    if need > 0:
                        put(self.backward, r, near, need)
        self.packed = {near} | ({len(order)} if at[len(order)] else set())
        assert max(at.values()) <= LANES
        per = CHUNK // LANES
        tiles = len(order) + (1 if at[len(order)] else 0)
        self.chunks = -(-tiles // per)
        self.back_chunks = -(-(near + 1) // per)
        self.near = near
        self.lanes = self.chunks * CHUNK
        self.back_lanes = self.back_chunks * CHUNK
        self.spare = [t for t in range(tiles, self.chunks * per)]


PLANS = [Plan(7, 1), Plan(6, 3), Plan(5, 5)]


def dot(left, right):
    return lax.dot_general(left, right, (((1,), (0,)), ((), ())), preferred_element_type=F32)


def dot_rows(left, right):
    return lax.dot_general(left, right, (((1,), (1,)), ((), ())), preferred_element_type=F32)


def lane_index():
    return lax.broadcasted_iota(jnp.int32, (8, LANES), 1)


def field_index():
    return lax.broadcasted_iota(jnp.int32, (8, LANES), 0)


def pack_kernel(state_ref, adjoint_ref, stiff_ref, pinned_ref, weave_ref, own_ref, low_ref, high_ref):
    lane, field = lane_index(), field_index()
    low = [jnp.zeros((8, LANES), F32) for _ in range(3)]
    high = [jnp.zeros((8, LANES), F32) for _ in range(3)]
    for row in range(TILE_ROWS):
        k0 = stiff_ref[0, row : row + 1, :]
        k1 = stiff_ref[1, row : row + 1, :]
        free = 1.0 - pinned_ref[0, row : row + 1, :].astype(F32)
        code = weave_ref[row : row + 1, :]
        first_sign = (2 * jnp.bitwise_and(code, 1) - 1).astype(F32)
        second_sign = (2 * jnp.right_shift(code, 1) - 1).astype(F32)
        cell = jnp.where(field == 5, 1.0, 0.0)
        for place, value in enumerate((k0, k1, first_sign, second_sign, free)):
            cell = jnp.where(field == place, value, cell)
        at = REACH * row
        here = (lane >= at) & (lane < at + REACH)
        for part, value in enumerate((state_ref[0, :, row, :], adjoint_ref[0, :, row, :], cell)):
            own_ref[row, 8 * part : 8 * part + 8, :] = value
            low[part] = jnp.where(here, pltpu.roll(value, at, 1) if at else value, low[part])
            shift = (at + REACH) % LANES
            high[part] = jnp.where(here, pltpu.roll(value, shift, 1), high[part])
    for part in range(3):
        low_ref[8 * part : 8 * part + 8, :] = low[part]
        high_ref[8 * part : 8 * part + 8, :] = high[part]


def roll(value, shift, axis):
    shift = shift % value.shape[axis]
    return pltpu.roll(value, shift, axis) if shift else value


def main_kernel(
    own_ref,
    left_ref,
    right_ref,
    below_ref,
    above_ref,
    far_below_ref,
    far_above_ref,
    w1t_ref,
    w1_ref,
    w2t_ref,
    w2_ref,
    w3t_ref,
    w3_ref,
    final_ref,
    adjoint_ref,
    grads_ref,
    state_a,
    state_b,
    later,
    adjoint,
    k0_ref,
    k1_ref,
    mask_ref,
    sign_ref,
    force_ref,
    ahead_ref,
    behind_ref,
    sum_ref,
    x0,
    x1,
    x2,
    slope_first0,
    slope_first1,
    slope_first2,
    slope_second0,
    slope_second1,
    slope_second2,
    act_first,
    act_second,
    friction,
    upstream,
    feature_back,
    back_first,
    back_second,
    total_second,
    total_first,
    total_third,
):
    lane, field = lane_index(), field_index()
    zero = jnp.zeros((8, LANES), F32)
    xs = (x0, x1, x2)
    slopes_first = (slope_first0, slope_first1, slope_first2)
    slopes_second = (slope_second0, slope_second1, slope_second2)
    place = field < 3
    speed = (field >= 3) & (field < 6)
    slide = field >= 6

    def beside(low, high, row):
        at = REACH * row
        out = jnp.where(lane < REACH, roll(high, -at, 1), 0.0)
        return jnp.where(lane >= LANES - REACH, roll(low, LANES - REACH - at, 1), out)

    for row in range(ALL_ROWS):
        e = row - FIRST
        if e < -TILE_ROWS:
            block, inside, near = far_below_ref, e + TILE_ROWS + 2, e + 2 * TILE_ROWS
        elif e < 0:
            block, inside, near = below_ref, e + TILE_ROWS, e + TILE_ROWS
        elif e < TILE_ROWS:
            block, inside, near = own_ref, e, e
        elif e < 2 * TILE_ROWS:
            block, inside, near = above_ref, e - TILE_ROWS, e - TILE_ROWS
        else:
            block, inside, near = far_above_ref, e - 2 * TILE_ROWS, e - 2 * TILE_ROWS
        for part in range(3 if -TILE_ROWS <= e < 2 * TILE_ROWS else 1):
            at = slice(8 * part, 8 * part + 8)
            if block is own_ref:
                low, high = left_ref[at, :], right_ref[at, :]
            elif block is far_below_ref or block is far_above_ref:
                low, high = block[2, at, :], block[3, at, :]
            else:
                low, high = block[TILE_ROWS, at, :], block[TILE_ROWS + 1, at, :]
            pair = (block[inside, at, :], beside(low, high, near))
            for half in range(2):
                value = pair[half]
                if part == 0:
                    state_a[row, half] = value
                elif part == 1:
                    adjoint[row, half] = value
                else:
                    k0_ref[row, half] = jnp.broadcast_to(value[0:1], (8, LANES))
                    k1_ref[row, half] = jnp.broadcast_to(value[1:2], (8, LANES))
                    mask_ref[row, half] = jnp.where(
                        place, 1.0, jnp.where(speed, value[4:5], value[5:6])
                    )
                    sign_ref[row, half] = jnp.where((field == 2) | (field == 3), value, 0.0)

    def across(pair, step):
        turned = [roll(value, -step, 1) for value in pair]
        edge = lane >= LANES - step if step > 0 else lane < -step
        return jnp.where(edge, turned[1], turned[0]), jnp.where(edge, turned[0], turned[1])

    def both(ref, row):
        return ref[row, 0], ref[row, 1]

    def gather(total, value, entry):
        _, at, width = entry
        turned = roll(value, at + width, 1)
        return jnp.where((lane >= at) & (lane < at + 2 * width), turned, total)

    def scatter(value, entry):
        _, at, width = entry
        turned = roll(value, -(at + width), 1)
        return jnp.where((lane < width) | (lane >= LANES - width), turned, 0.0)

    def tile_lanes(tile):
        return slice(tile * LANES, (tile + 1) * LANES)

    gravity = jnp.where(field == 5, -GRAV, 0.0)
    keep = jnp.where(speed, DAMP, 1.0)

    def forward(k, state, target):
        plan = PLANS[k]
        x_ref = xs[k]
        moved = span((8, 6, 0)[k])
        packed = {tile: [zero, zero] for tile in plan.packed}
        for row in sorted(set(moved) | set(span(plan.reach))):
            here, up, down = both(state, row), both(state, row + 1), both(state, row - 1)
            right, left = across(here, 1), across(here, -1)
            update = row in moved
            if update:
                up2, down2 = both(state, row + 2), both(state, row - 2)
                right2, left2 = across(here, 2), across(here, -2)
            for half in range(2):
                s = here[half]
                twice = 2.0 * s
                lap_rows = up[half] + down[half] - twice
                lap_columns = right[half] + left[half] - twice
                slope_rows = 0.5 * (up[half] - down[half])
                slope_columns = 0.5 * (right[half] - left[half])
                if row in plan.tile:
                    mixed = jnp.where(field == 0, slope_rows, sign_ref[row, half])
                    mixed = jnp.where(field == 1, slope_columns, mixed)
                    mixed = jnp.where(field == 6, lap_rows, mixed)
                    mixed = jnp.where(field == 7, lap_columns, mixed)
                    if half == 0:
                        x_ref[:, tile_lanes(plan.tile[row])] = jnp.concatenate([s, mixed], axis=0).astype(BF16)
                    else:
                        for table in (plan.forward, plan.backward):
                            if row in table and (table is plan.forward or table[row] != plan.forward.get(row)):
                                entry = table[row]
                                old = packed[entry[0]]
                                packed[entry[0]] = [gather(old[0], s, entry), gather(old[1], mixed, entry)]
                if update and (half == 0 or k < 2):
                    bend = (up2[half] + down2[half] + right2[half] + left2[half]) - 4.0 * (
                        up[half] + down[half] + right[half] + left[half]
                    )
                    bend = bend + 12.0 * s
                    pull = k0_ref[row, half] * lap_rows + k1_ref[row, half] * lap_columns - KB * bend
                    turn = KC * jnp.where(field == 6, slope_rows, jnp.where(field == 7, slope_columns, 0.0))
                    force = roll(pull, 3, 0) + roll(turn, 5, 0) + gravity
                    rate = KS * jnp.where(field == 6, lap_rows, lap_columns)
                    change = jnp.where(speed, force, jnp.where(slide, rate, 0.0))
                    later[row, half] = keep * s + DT * change
        for tile, (top, bottom) in packed.items():
            x_ref[:, tile_lanes(tile)] = jnp.concatenate([top, bottom], axis=0).astype(BF16)
        for tile in plan.spare:
            x_ref[:, tile_lanes(tile)] = jnp.zeros((16, LANES), BF16)

        def network(c, own, saved):
            at = pl.ds(pl.multiple_of(c * CHUNK, CHUNK), CHUNK)
            z = dot(w1t_ref[...], x_ref[:, at])
            bent = jnp.tanh(z)
            part = z * bent
            act = (z + part).astype(BF16)
            if saved:
                slopes_first[k][:, at] = (1.0 + bent) * (1.0 + (z - part))
            if own:
                act_first[k, :, at] = act
            z = dot(w2t_ref[...], act)
            bent = jnp.tanh(z)
            part = z * bent
            act = (z + part).astype(BF16)
            if saved:
                slopes_second[k][:, at] = (1.0 + bent) * (1.0 + (z - part))
            if own:
                act_second[k, :, at] = act
            friction[:, at] = dot(w3t_ref[...], act)

        def loop(start, stop, own, saved):
            if stop > start:

                def body(c, carry):
                    network(c, own, saved)
                    return carry

                lax.fori_loop(start, stop, body, 0)

        loop(0, OWN // CHUNK, True, True)
        loop(OWN // CHUNK, plan.back_chunks, False, True)
        loop(plan.back_chunks, plan.chunks, False, False)
        for row in moved:
            for half in range(2 if k < 2 else 1):
                value = later[row, half]
                if half == 0 and row in plan.tile:
                    value = value - DT * friction[:, tile_lanes(plan.tile[row])]
                if half == 1 and row in plan.forward:
                    entry = plan.forward[row]
                    value = value - DT * scatter(friction[:, tile_lanes(entry[0])], entry)
                value = mask_ref[row, half] * value
                value = value + jnp.where(place, DT * roll(value, 5, 0), 0.0)
                if k < 2:
                    target[row, half] = value
                else:
                    final_ref[0, :, row - FIRST, :] = value

    forward(0, state_a, state_b)
    forward(1, state_b, state_a)
    forward(2, state_a, None)

    def backward(k):
        plan = PLANS[k]
        inner, middle, outer = plan.back - 1, plan.back, plan.back + 1
        packed = zero
        for row in span(middle):
            for half in range(2):
                value = jnp.where(slide, -DT * adjoint[row, half], 0.0)
                if half == 0:
                    upstream[:, tile_lanes(plan.tile[row])] = jnp.concatenate([value, zero], axis=0).astype(BF16)
                elif row in plan.backward:
                    packed = gather(packed, value, plan.backward[row])
        upstream[:, tile_lanes(plan.near)] = jnp.concatenate([packed, zero], axis=0).astype(BF16)
        for tile in range(plan.near + 1, plan.back_chunks * (CHUNK // LANES)):
            upstream[:, tile_lanes(tile)] = jnp.zeros((16, LANES), BF16)

        def network(c, own):
            at = pl.ds(pl.multiple_of(c * CHUNK, CHUNK), CHUNK)
            back = (dot(w3_ref[...], upstream[:, at]) * slopes_second[k][:, at]).astype(BF16)
            if own:
                back_second[:, at] = back
            back = (dot(w2_ref[...], back) * slopes_first[k][:, at]).astype(BF16)
            if own:
                back_first[:, at] = back
            feature_back[:, at] = dot(w1_ref[...], back)

        def loop(start, stop, own):
            def body(c, carry):
                network(c, own)
                return carry

            lax.fori_loop(start, stop, body, 0)

        loop(0, OWN // CHUNK, True)
        loop(OWN // CHUNK, plan.back_chunks, False)
        second = dot_rows(act_first[k], back_second[...])
        first = dot_rows(xs[k][:, 0:OWN], back_first[...])
        third = dot_rows(upstream[:, 0:OWN], act_second[k])
        if k == 2:
            total_second[...], total_first[...], total_third[...] = second, first, third
        else:
            total_second[...] += second
            total_first[...] += first
            total_third[...] += third

        for row in span(outer):
            for half in range(2):
                q = adjoint[row, half]
                total = mask_ref[row, half] * (q + DT * roll(q, 3, 0))
                force_ref[row, half] = jnp.where(place, DT * roll(total, 5, 0), 0.0)
                if distance(row) <= inner:
                    sum_ref[row, half] = jnp.where(speed, DAMP * total, q)
        for row in span(middle):
            force = both(force_ref, row)
            high, low = [], []
            for half in range(2):
                q, g = adjoint[row, half], force[half]
                if half == 0:
                    at = tile_lanes(plan.tile[row])
                    straight, mixed = feature_back[0:8, at], feature_back[8:16, at]
                elif row in plan.backward:
                    entry = plan.backward[row]
                    at = tile_lanes(entry[0])
                    straight, mixed = scatter(feature_back[0:8, at], entry), scatter(feature_back[8:16, at], entry)
                else:
                    straight, mixed = zero, zero
                carried = DT * KS * q + mixed
                by_rows = k0_ref[row, half] * g + jnp.where(field == 6, carried, 0.0)
                by_columns = k1_ref[row, half] * g + jnp.where(field == 7, carried, 0.0)
                tilt = 0.5 * jnp.where(slide, KC * roll(g, 6, 0), mixed)
                tilt_rows = jnp.where((field == 0) | (field == 6), tilt, 0.0)
                tilt_columns = jnp.where((field == 1) | (field == 7), tilt, 0.0)
                ahead_ref[row, half] = by_rows + 4.0 * KB * g - tilt_rows
                behind_ref[row, half] = by_rows + 4.0 * KB * g + tilt_rows
                high.append(by_columns + 4.0 * KB * g - tilt_columns)
                low.append(by_columns + 4.0 * KB * g + tilt_columns)
                if distance(row) <= inner:
                    center = -2.0 * (by_rows + by_columns) - 12.0 * KB * g
                    sum_ref[row, half] = sum_ref[row, half] + straight + center
            if distance(row) <= inner:
                right, left = across(high, 1), across(low, -1)
                right2, left2 = across(force, 2), across(force, -2)
                for half in range(2):
                    sideways = right[half] + left[half] - KB * (right2[half] + left2[half])
                    sum_ref[row, half] = sum_ref[row, half] + sideways
        for row in span(inner):
            for half in range(2 if k > 0 else 1):
                value = sum_ref[row, half] + ahead_ref[row + 1, half] + behind_ref[row - 1, half]
                value = value - KB * (force_ref[row + 2, half] + force_ref[row - 2, half])
                if k > 0:
                    adjoint[row, half] = jnp.where(slide, mask_ref[row, half] * value, value)
                else:
                    adjoint_ref[0, :, row - FIRST, :] = value

    backward(2)
    backward(1)
    backward(0)

    small = total_first[...]
    third = total_third[0:8, :]
    row_index = lax.broadcasted_iota(jnp.int32, (8, HID), 0)
    top = jnp.where(row_index < 2, pltpu.roll(third, 2, 0), small[0:8])
    bottom = small[8:16]
    for c in range(HID // 8):
        grads_ref[c, 0:8, :] = total_second[8 * c : 8 * c + 8, 0:LANES]
        grads_ref[c, 8:16, :] = total_second[8 * c : 8 * c + 8, LANES:]
        line = (top if c < 16 else bottom)[(c // 2) % 8 : (c // 2) % 8 + 1, (c % 2) * LANES : (c % 2 + 1) * LANES]
        grads_ref[c, 16:24, :] = jnp.broadcast_to(line, (8, LANES))


def run_main(*operands):
    rows = (ALL_ROWS, 2, 8, LANES)
    scratch = [pltpu.VMEM(rows, F32) for _ in range(12)]
    scratch += [pltpu.VMEM((16, plan.lanes), BF16) for plan in PLANS]
    scratch += [pltpu.VMEM((HID, plan.back_lanes), F32) for plan in PLANS] * 2
    scratch += [pltpu.VMEM((3, HID, OWN), BF16)] * 2
    scratch += [
        pltpu.VMEM((8, PLANS[0].lanes), F32),
        pltpu.VMEM((16, PLANS[2].back_lanes), BF16),
        pltpu.VMEM((16, PLANS[2].back_lanes), F32),
        pltpu.VMEM((HID, OWN), BF16),
        pltpu.VMEM((HID, OWN), BF16),
        pltpu.VMEM((HID, HID), F32),
        pltpu.VMEM((16, HID), F32),
        pltpu.VMEM((16, HID), F32),
    ]
    return pl.pallas_call(
        main_kernel,
        out_shape=(
            jax.ShapeDtypeStruct((1, 8, TILE_ROWS, LANES), F32),
            jax.ShapeDtypeStruct((1, 8, TILE_ROWS, LANES), F32),
            jax.ShapeDtypeStruct((HID // 8, 24, LANES), F32),
        ),
        scratch_shapes=scratch,
        name="substeps",
    )(*operands)


def run_pack(*operands):
    return pl.pallas_call(
        pack_kernel,
        out_shape=(
            jax.ShapeDtypeStruct((TILE_ROWS, 24, LANES), F32),
            jax.ShapeDtypeStruct((24, LANES), F32),
            jax.ShapeDtypeStruct((24, LANES), F32),
        ),
        name="pack_tile",
    )(*operands)


def shift(value, axis, step):
    count = lax.axis_size(axis)
    return lax.ppermute(value, axis, [(i, i + step) for i in range(count) if 0 <= i + step < count])


def sum_everywhere(part):
    plane, column = lax.axis_size(PLANE), lax.axis_size(COLUMN)
    part = jnp.sum(lax.all_to_all(part, PLANE, 0, 0, tiled=True), axis=0)
    part = jnp.broadcast_to(part, (column,) + part.shape)
    part = jnp.sum(lax.all_to_all(part, COLUMN, 0, 0, tiled=True), axis=0)
    part = jnp.broadcast_to(part, (plane,) + part.shape)
    return lax.all_to_all(part, PLANE, 0, 0, tiled=True)


def finish_kernel(scale, flat_ref, first_ref, second_ref, third_ref):
    for c in range(HID // 8):
        second_ref[8 * c : 8 * c + 8, 0:LANES] = flat_ref[c, 0:8, :] * scale
        second_ref[8 * c : 8 * c + 8, LANES:] = flat_ref[c, 8:16, :] * scale
    for half in range(2):
        at = slice(half * LANES, (half + 1) * LANES)
        for f, row in enumerate((6, 7, 3, 4, 5, 14, 15, 8, 9, 2, 10, 11)):
            first_ref[f : f + 1, at] = flat_ref[2 * row + half, 16:17, :] * scale
        for f in range(2):
            third_ref[f : f + 1, at] = flat_ref[2 * f + half, 16:17, :] * scale


def shards(state, adjoint, stiffness, pinned, weave, first_weight, second_weight, third_weight):
    own, low_edge, high_edge = run_pack(state, adjoint, stiffness, pinned, weave)
    left = shift(high_edge, WEFT, 1)
    right = shift(low_edge, WEFT, -1)
    wide = jnp.concatenate([own, left[None], right[None]], axis=0)
    sides = wide[TILE_ROWS:, 0:8]
    below = shift(wide, WARP, 1)
    above = shift(wide, WARP, -1)
    far_below = shift(jnp.concatenate([own[TILE_ROWS - 2 :, 0:8], sides], axis=0), WARP, 2)
    far_above = shift(jnp.concatenate([own[0:2, 0:8], sides], axis=0), WARP, -2)

    blank = jnp.zeros((2, HID), BF16)
    w = first_weight
    w1 = jnp.concatenate(
        [blank, w[9:10], w[2:5], w[0:2], w[7:9], w[10:12], blank, w[5:7]], axis=0
    )
    half = jnp.asarray(0.5, BF16)
    w1t = (half * w1).T
    w2 = half * second_weight
    w2t = w2.T
    w3t = jnp.pad(third_weight.T, ((6, 0), (0, 0)))
    w3 = jnp.pad(half * third_weight, ((0, 0), (6, 8)))
    final_state, state_adjoint, grads = run_main(
        own, left, right, below, above, far_below, far_above, w1t, w1, w2t, w2, w3t, w3
    )
    flat = sum_everywhere(grads)
    cells = OWN * lax.axis_size(WARP) * lax.axis_size(WEFT)
    first, second, third = pl.pallas_call(
        functools.partial(finish_kernel, float(cells) ** -0.5),
        out_shape=(
            jax.ShapeDtypeStruct((12, HID), F32),
            jax.ShapeDtypeStruct((HID, HID), F32),
            jax.ShapeDtypeStruct((2, HID), F32),
        ),
        name="unpack_grads",
    )(flat)
    return final_state, state_adjoint, first, second, third.T


def factors(mesh):
    warp, weft = mesh.shape["warp"], mesh.shape["weft"]
    zlo = 4 if weft % 4 == 0 else 1
    x = 4 if warp % 8 == 0 else 1
    core = 2 if warp % 2 == 0 else 1
    return (warp // (x * core), x, core, weft // zlo, zlo)


def solution(mesh):
    fine = Mesh(mesh.devices.reshape(factors(mesh)), WARP + WEFT)
    field = P(None, None, WARP, WEFT)
    placed = (field, field, P(None, WARP, WEFT), P(None, WARP, WEFT), P(WARP, WEFT), P(), P(), P())
    return jax.shard_map(
        shards,
        mesh=fine,
        in_specs=placed,
        out_specs=(field, field, P(), P(), P()),
        check_vma=False,
    )
```

time: 323 us -> 140 us (0.43)
  starting transfers between devices: 147 us -> 19.6 us
  blocking collectives: 0 us -> 73.4 us
  waiting for transfers between devices: 70.7 us -> 1.88 us
  matrix products: 50.6 us -> 0 us
  Pallas kernels: 0 us -> 37.8 us
  local copies, waits for them, and re-layouts: 36.1 us -> 5.11 us
  other arithmetic: 13.2 us -> 0.76 us
    all_to_all x0 -> x3, blocking collectives: none -> 73.4 us  [the longest x1 27.6 us: sum_everywhere(): part = jnp.sum(lax.all_to_all(part, COLUMN, 0, 0, tiled=True), axis=0)]
    ppermute x28 -> x6, starting transfers between devices: 91.7 us -> 19.6 us  [shift(): lax.ppermute(value, axis, [(i, i + step) for i in range(count) if 0 <= i...]
    all_to_all x3 -> x0, starting transfers between devices: 55.5 us -> none  [the longest x1 37 us: sum_everywhere(): part = jnp.sum(lax.all_to_all(flat, PLANE, 0, 0, tiled=True), axis=0)]
    dot_general x60 -> x0, matrix products: 50.6 us -> none  [the longest x24 27.1 us: contract(): lax.dot_general(left, right, (((0,), (0,)), ((), ())), preferred_element_...]
    pallas_call x0 -> x3, Pallas kernels: none -> 37.8 us  [the longest x1 34.5 us: run_main(): pl.pallas_call(main_kernel, out_shape=(jax.ShapeDtypeStruct((1, 8, TILE_R...]
    ppermute x28 -> x6, waiting for transfers between devices: 39.3 us -> 1.88 us  [shift(): lax.ppermute(value, axis, [(i, i + step) for i in range(count) if 0 <= i...]
    all_to_all x3 -> x0, waiting for transfers between devices: 31.4 us -> none  [the longest x1 12.4 us: sum_everywhere(): part = jnp.sum(lax.all_to_all(part, COLUMN, 0, 0, tiled=True), axis=0)]
    slice x19 -> x4, local copies, waits for them, and re-layouts: 30.9 us -> 0.02 us  [the longest x1 0.01 us: shards(): w[5:7]]
  transfers between devices with their start and end apart: 31 -> 6, of which waited for: 13 -> 1; matrix products, arithmetic and copies ran while one was open for 9% -> 3% of each run, Pallas kernels for 0% -> 0%
where the time goes in v2:
time: 140 us
  blocking collectives  73.4 us (52%)
  Pallas kernels  37.8 us (27%)
  starting transfers between devices  19.6 us (14%)
  local copies, waits for them, and re-layouts  5.11 us (4%)
  waiting for transfers between devices  1.88 us (1%)
    pallas_call x1, Pallas kernels, run_main(): pl.pallas_call(main_kernel, out_shape=(jax.ShapeDtypeStruct((1, 8, TILE_R...  34.5 us
    all_to_all x1, blocking collectives, sum_everywhere(): part = jnp.sum(lax.all_to_all(part, COLUMN, 0, 0, tiled=True), axis=0)  27.6 us
    all_to_all x1, blocking collectives, sum_everywhere(): part = jnp.sum(lax.all_to_all(part, PLANE, 0, 0, tiled=True), axis=0)  27.5 us
    ppermute x6, starting transfers between devices, shift(): lax.ppermute(value, axis, [(i, i + step) for i in range(count) if 0 <= i...  19.6 us
    all_to_all x1, blocking collectives, sum_everywhere(): return lax.all_to_all(part, PLANE, 0, 0, tiled=True)  18.3 us
  transfers between devices with their start and end apart: 6, of which 1 were waited for; matrix products, arithmetic and copies ran while one was open for 3% of the time, Pallas kernels for 0%

profile of v2, /device:TPU:1, one launch (start us, length us, event | category | flops | bytes accessed | tf_op | source)
XLA Modules:
  0.0 139.5 jit_solution(203146062203776507)
XLA Ops:
  0.6 0.0 copy-start.1
  0.6 1.6 %pack_tile.1 = (f32[8,24,128]{2,1,0:T(8,128)}, f32[24,128]{1,0:T(8,128)}, f32[24,128]{1,0:T(8,128)}) custom-call(f32[1,8,8,128]{3,2,1,0:T(8,128)} %state_ref.1, f32[1,8,8,128]{3,2,1,0:T(8,128)} %adjoint_ref.1, f32[2,8,128]{2,1,0:T(8,128)} %stiff_ref.1, s32[1,8,128]{2,1,0:T(8,128)} %pinned_ref.1, s32[8,128]{1,0:T(8,128)} %weave_ref.1), custom_call_target="tpu_custom_call" | custom-call | tf_op jit(solution)/shard_map/pack_tile/pallas_call | solution.py:495
  2.2 4.4 %collective-permute-start = (f32[24,128]{1,0:T(8,128)}, f32[24,128]{1,0:T(8,128)S(1)}, u32[]{:S(2)}, u32[]{:S(2)}) collective-permute-start(f32[24,128]{1,0:T(8,128)} %get-tuple-element.15), channel_id=1, source_target_pairs={{0,1},{1,2},{2,3},{3,4},{4,5},{5,6},{6,7},{7,8},{8,9},{9,10},{10,1... | collective-permute-start | bytes 36872 | tf_op jit(solution)/shard_map/ppermute | solution.py:508
  6.6 0.0 copy-start
  6.6 1.4 %collective-permute-start.1 = (f32[24,128]{1,0:T(8,128)}, f32[24,128]{1,0:T(8,128)S(1)}, u32[]{:S(2)}, u32[]{:S(2)}) collective-permute-start(f32[24,128]{1,0:T(8,128)} %get-tuple-element.16), channel_id=1, source_target_pairs={{1,0},{2,1},{3,2},{4,3},{5,4},{6,5},{7,6},{8,7},{9,8},{10,9},{11,1... | collective-permute-start | bytes 36872 | tf_op jit(solution)/shard_map/ppermute | solution.py:508
  8.0 0.8 copy.19
  8.8 0.0 copy-done
  8.9 0.0 copy-done.1
  8.9 0.0 copy-start.9
  8.9 0.7 broadcast_multiply_fusion
  9.6 0.0 copy-done.9
  9.6 0.1 concatenate.19.w1_ref
  9.7 0.0 copy-start.6
  9.7 0.0 collective-permute-done.left_ref
  9.7 0.0 copy-start.4
  9.7 1.9 %collective-permute-done.1.right_ref = f32[24,128]{1,0:T(8,128)S(1)} collective-permute-done((f32[24,128]{1,0:T(8,128)}, f32[24,128]{1,0:T(8,128)S(1)}, u32[]{:S(2)}, u32[]{:S(2)}) %collective-permute-start.1) | collective-permute-done | bytes 12320 | tf_op jit(solution)/shard_map/ppermute | solution.py:508
  11.6 0.0 copy-start.5
  11.6 6.7 %collective-permute-start.3 = (f32[10,24,128]{2,1,0:T(8,128)S(1)}, f32[10,24,128]{2,1,0:T(8,128)S(1)}, u32[]{:S(2)}, u32[]{:S(2)}) collective-permute-start(f32[10,24,128]{2,1,0:T(8,128)S(1)} %pad_maximum_fusion), channel_id=1, source_target_pairs={{16,0},{32,16},{48,32},{64,48},{80,64},{96,80},{112,96},{128,112},... | collective-permute-start | bytes 368648 | tf_op jit(solution)/shard_map/ppermute | solution.py:508
  18.2 1.9 %collective-permute-start.2 = (f32[10,24,128]{2,1,0:T(8,128)S(1)}, f32[10,24,128]{2,1,0:T(8,128)S(1)}, u32[]{:S(2)}, u32[]{:S(2)}) collective-permute-start(f32[10,24,128]{2,1,0:T(8,128)S(1)} %pad_maximum_fusion), channel_id=1, source_target_pairs={{0,16},{16,32},{32,48},{48,64},{64,80},{80,96},{96,112},{112,128},... | collective-permute-start | bytes 368648 | tf_op jit(solution)/shard_map/ppermute | solution.py:508
  20.2 0.0 copy-done.4
  20.2 0.0 copy-done.5
  20.2 1.3 collective-permute-start.5
  21.5 4.0 %collective-permute-start.4 = (f32[4,8,128]{2,1,0:T(8,128)S(1)}, f32[4,8,128]{2,1,0:T(8,128)S(1)}, u32[]{:S(2)}, u32[]{:S(2)}) collective-permute-start(f32[4,8,128]{2,1,0:T(8,128)S(1)} %get-tuple-element.28), channel_id=1, source_target_pairs={{0,32},{16,48},{32,64},{48,80},{64,96},{80,112},{96,128},{112,144}... | collective-permute-start | bytes 49160 | tf_op jit(solution)/shard_map/ppermute | solution.py:508
  25.5 0.0 copy-done.6
  25.5 0.0 copy-start.10
  25.5 0.7 copy-done.10
  26.2 0.6 pad.8.w3t_ref
  26.8 0.7 copy.21.w1t_ref
  27.5 0.7 pad.9.w3_ref
  28.2 0.7 copy.22.w2t_ref
  29.0 0.0 collective-permute-done.5.far_above_ref
  29.0 0.0 copy-start.7
  29.0 0.0 collective-permute-done.4.far_below_ref
  29.0 0.0 copy-start.8
  29.0 0.0 collective-permute-done.3.above_ref
  29.0 0.0 copy-start.2
  29.0 0.0 collective-permute-done.2.below_ref
  29.1 0.0 copy-start.3
  29.1 0.5 copy-done.7
  29.6 0.0 copy-done.8
  29.6 0.1 copy-done.2
  29.7 0.0 copy-done.3
  29.7 34.5 %substeps.1 = (f32[1,8,8,128]{3,2,1,0:T(8,128)}, f32[1,8,8,128]{3,2,1,0:T(8,128)}, f32[32,24,128]{2,1,0:T(8,128)}) custom-call(f32[8,24,128]{2,1,0:T(8,128)} %get-tuple-element.14.own_ref, f32[24,128]{1,0:T(8,128)} %copy-done.4, f32[24,128]{1,0:T(8,128)} %copy-done.5, f32[10,24,128]{2,1,0:T(8,128)} %copy-done.3, f32[10,24,128]{2,1,0:T(8,128)} %copy-done.2, ...), custom_call_target="tpu_custom_call" | custom-call | tf_op jit(solution)/shard_map/substeps/pallas_call | solution.py:482
  64.2 27.5 %all_to_all.15 = f32[32,24,128]{2,1,0:T(8,128)S(1)} all-to-all(f32[32,24,128]{2,1,0:T(8,128)} %get-tuple-element.19), channel_id=1, replica_groups=mesh['zhi'=4,'x'=4,'core'=2,'y'=4,'zlo'=4] {'x','core','y'}, dimensions={0} | all-to-all | bytes 786432 | tf_op jit(solution)/shard_map/all_to_all | solution.py:513
  91.8 27.6 %all_to_all.16 = f32[16,24,128]{2,1,0:T(8,128)S(1)} all-to-all(f32[16,24,128]{2,1,0:T(8,128)S(1)} %broadcast_in_dim.18), channel_id=1, replica_groups=mesh['zhi'=4,'x'=4,'core'=2,'y'=4,'zlo'=4] {'zhi','zlo'}, dimensions={0} | all-to-all | bytes 393216 | tf_op jit(solution)/shard_map/all_to_all | solution.py:515
  119.5 18.3 %all_to_all.17.flat_ref = f32[32,24,128]{2,1,0:T(8,128)} all-to-all(f32[32,24,128]{2,1,0:T(8,128)S(1)} %broadcast_in_dim.19), channel_id=1, replica_groups=mesh['zhi'=4,'x'=4,'core'=2,'y'=4,'zlo'=4] {'x','core','y'}, dimensions={0} | all-to-all | bytes 786432 | tf_op jit(solution)/shard_map/all_to_all | solution.py:517
  137.8 1.7 %unpack_grads.1 = (f32[12,256]{1,0:T(8,128)}, f32[256,256]{1,0:T(8,128)}, f32[2,256]{1,0:T(2,128)}) custom-call(f32[32,24,128]{2,1,0:T(8,128)} %all_to_all.17.flat_ref), custom_call_target="tpu_custom_call" | custom-call | tf_op jit(solution)/shard_map/unpack_grads/pallas_call | solution.py:559
  (13 shorter events, 0.2 us)
Async XLA Ops:
  0.6 8.2 %copy-start.1 = (bf16[256,256]{1,0:T(8,128)(2,1)S(1)}, bf16[256,256]{1,0:T(8,128)(2,1)}, u32[]{:S(2)}) copy-start(bf16[256,256]{1,0:T(8,128)(2,1)} %param.14) | copy-start | bytes 393220
  2.2 7.5 %collective-permute-start = (f32[24,128]{1,0:T(8,128)}, f32[24,128]{1,0:T(8,128)S(1)}, u32[]{:S(2)}, u32[]{:S(2)}) collective-permute-start(f32[24,128]{1,0:T(8,128)} %get-tuple-element.15), channel_id=1, source_target_pairs={{0,1},{1,2},{2,3},{3,4},{4,5},{5,6},{6,7},{7,8},{8,9},{9,10},{10,1... | collective-permute-start | bytes 36872 | tf_op jit(solution)/shard_map/ppermute | solution.py:508
  6.6 2.3 %copy-start = (f32[8,24,128]{2,1,0:T(8,128)S(1)}, f32[8,24,128]{2,1,0:T(8,128)}, u32[]{:S(2)}) copy-start(f32[8,24,128]{2,1,0:T(8,128)} %get-tuple-element.14.own_ref) | copy-start | bytes 294916
  6.6 5.0 %collective-permute-start.1 = (f32[24,128]{1,0:T(8,128)}, f32[24,128]{1,0:T(8,128)S(1)}, u32[]{:S(2)}, u32[]{:S(2)}) collective-permute-start(f32[24,128]{1,0:T(8,128)} %get-tuple-element.16), channel_id=1, source_target_pairs={{1,0},{2,1},{3,2},{4,3},{5,4},{6,5},{7,6},{8,7},{9,8},{10,9},{11,1... | collective-permute-start | bytes 36872 | tf_op jit(solution)/shard_map/ppermute | solution.py:508
  8.9 0.7 copy-start.9
  9.7 15.8 %copy-start.6 = (bf16[16,256]{1,0:T(8,128)(2,1)}, bf16[16,256]{1,0:T(8,128)(2,1)S(1)}, u32[]{:S(2)}) copy-start(bf16[16,256]{1,0:T(8,128)(2,1)S(1)} %concatenate.19.w1_ref) | copy-start | bytes 24580
  9.7 10.5 %copy-start.4 = (f32[24,128]{1,0:T(8,128)}, f32[24,128]{1,0:T(8,128)S(1)}, u32[]{:S(2)}) copy-start(f32[24,128]{1,0:T(8,128)S(1)} %collective-permute-done.left_ref) | copy-start | bytes 36868
  11.6 8.6 %copy-start.5 = (f32[24,128]{1,0:T(8,128)}, f32[24,128]{1,0:T(8,128)S(1)}, u32[]{:S(2)}) copy-start(f32[24,128]{1,0:T(8,128)S(1)} %collective-permute-done.1.right_ref) | copy-start | bytes 36868
  11.6 17.4 %collective-permute-start.3 = (f32[10,24,128]{2,1,0:T(8,128)S(1)}, f32[10,24,128]{2,1,0:T(8,128)S(1)}, u32[]{:S(2)}, u32[]{:S(2)}) collective-permute-start(f32[10,24,128]{2,1,0:T(8,128)S(1)} %pad_maximum_fusion), channel_id=1, source_target_pairs={{16,0},{32,16},{48,32},{64,48},{80,64},{96,80},{112,96},{128,112},... | collective-permute-start | bytes 368648 | tf_op jit(solution)/shard_map/ppermute | solution.py:508
  18.2 10.8 %collective-permute-start.2 = (f32[10,24,128]{2,1,0:T(8,128)S(1)}, f32[10,24,128]{2,1,0:T(8,128)S(1)}, u32[]{:S(2)}, u32[]{:S(2)}) collective-permute-start(f32[10,24,128]{2,1,0:T(8,128)S(1)} %pad_maximum_fusion), channel_id=1, source_target_pairs={{0,16},{16,32},{32,48},{48,64},{64,80},{80,96},{96,112},{112,128},... | collective-permute-start | bytes 368648 | tf_op jit(solution)/shard_map/ppermute | solution.py:508
  20.2 8.8 %collective-permute-start.5 = (f32[4,8,128]{2,1,0:T(8,128)S(1)}, f32[4,8,128]{2,1,0:T(8,128)S(1)}, u32[]{:S(2)}, u32[]{:S(2)}) collective-permute-start(f32[4,8,128]{2,1,0:T(8,128)S(1)} %get-tuple-element.27), channel_id=1, source_target_pairs={{32,0},{48,16},{64,32},{80,48},{96,64},{112,80},{128,96},{144,112}... | collective-permute-start | bytes 49160 | tf_op jit(solution)/shard_map/ppermute | solution.py:508
  21.5 7.5 %collective-permute-start.4 = (f32[4,8,128]{2,1,0:T(8,128)S(1)}, f32[4,8,128]{2,1,0:T(8,128)S(1)}, u32[]{:S(2)}, u32[]{:S(2)}) collective-permute-start(f32[4,8,128]{2,1,0:T(8,128)S(1)} %get-tuple-element.28), channel_id=1, source_target_pairs={{0,32},{16,48},{32,64},{48,80},{64,96},{80,112},{96,128},{112,144}... | collective-permute-start | bytes 49160 | tf_op jit(solution)/shard_map/ppermute | solution.py:508
  25.5 0.7 copy-start.10
  29.0 0.6 copy-start.7
  29.0 0.6 copy-start.8
  29.0 0.7 copy-start.2
  29.1 0.7 copy-start.3
